TPU v7x, 256 devices: a whole 4x4x8 slice. The times are simulated.
256 devices in a mesh: tower: 64 (over x, y, z_hi, core), member: 4 (over z_lo).
Axes of the slice: x: 4, y: 4, z: 8 (z_hi: 2, z_lo: 4; z = z_hi * 4 + z_lo), core: 2. Of those that a mesh axis runs over, the one named last changes fastest.
Arguments:
- slabs: bfloat16 [64, 1024, 4096], P('tower', None, 'member'), may hold values from -6 to 6
- cross_down: bfloat16 [64, 2, 4096, 512], P('tower', None, None, 'member'), may hold values from -0.09375 to 0.09375
- cross_up: bfloat16 [64, 2, 4096, 512], P('tower', None, None, 'member'), may hold values from -0.25 to 0.25
- cross_bias: float32 [64, 2, 4096], P('tower'), may hold values from -3 to 3
- projector: bfloat16 [64, 4096, 256], P('tower'), may hold values from -0.09375 to 0.09375
- placement: int32 [64, 32], P('tower'), may hold values from 0 to 31, each once within a row
- owner: int32 [4, 256], replicated, may hold values from 0 to 255, each once within a row
- inter_grad: bfloat16 [1024, 16384], P(('tower', 'member')), may hold values from -6 to 6
Outputs:
- interactions: float32 [1024, 16384], P(('tower', 'member'))
- slab_grad: bfloat16 [64, 1024, 4096], P('tower', None, 'member')
Inputs may be any that keep to these rules, and one draw needn't show every extreme that they name: Each row of placement names every feature of its tower once. Each row of owner names every sample of its block once.
All inputs are finite; a program needn't handle non-finite values.
Results may differ from a plain program's by a relative error of at most 0.018.
Values may be sent and summed in bfloat16 or wider, within the bound.
A program may use at most 128 MiB of HBM per device.

v0:
```python
import jax
import jax.numpy as jnp
from jax import lax
from jax.sharding import PartitionSpec as P


def side_by_side(arrays, axis, dim, along):
    both = jnp.concatenate(arrays, axis=along)
    filled, at, finished = (lax.all_gather(both, axis, axis=dim, tiled=True), 0, [])
    for a in arrays:
        finished.append(lax.slice_in_dim(filled, at, at + a.shape[along], axis=along))
        at += a.shape[along]
    return tuple(finished)


def per_device(slabs, cross_down, cross_up, cross_bias, projector, placement, owner, inter_grad):
    gathered = lax.all_to_all(slabs, "member", split_axis=1, concat_axis=2, tiled=True)
    row_count = gathered.shape[1]
    full_width = gathered.shape[2]
    features = placement.shape[1]
    slot_width = full_width // features
    depth_count = cross_down.shape[1]
    order = placement[0]
    inputs = (
        gathered[0]
        .reshape(row_count, features, slot_width)[:, order]
        .reshape(row_count, full_width)
    )
    inputs_f = inputs.astype(jnp.float32)
    biases = cross_bias[0]
    whole_down, whole_up = side_by_side((cross_down, cross_up), "member", 3, 0)
    current = inputs
    scales = []
    for depth in range(depth_count):
        hidden = jnp.dot(current, whole_down[0, depth], preferred_element_type=jnp.float32).astype(
            jnp.bfloat16
        )
        scale_now = (
            jnp.dot(hidden, whole_up[0, depth].T, preferred_element_type=jnp.float32)
            + biases[depth]
        )
        scales.append(scale_now)
        current = (inputs_f * scale_now + current.astype(jnp.float32)).astype(jnp.bfloat16)
    vector = jnp.dot(current, projector[0], preferred_element_type=jnp.float32).astype(jnp.bfloat16)
    own_row = lax.dynamic_index_in_dim(owner, lax.axis_index("member"), 0, keepdims=False)
    ordered = vector[own_row]
    owned = lax.all_to_all(ordered[:, None, :], "tower", split_axis=0, concat_axis=1, tiled=True)
    owned_rows = owned.shape[0]
    tower_count = owned.shape[1]
    owned_f = owned.reshape(owned_rows, -1, slot_width).astype(jnp.float32)
    vector_count = owned_f.shape[1]
    table = jnp.einsum("bie,bje->bij", owned_f, owned_f) / slot_width
    interactions = table.reshape(owned_rows, vector_count * vector_count)
    cotangent = inter_grad.astype(jnp.float32).reshape(owned_rows, vector_count, vector_count)
    symmetric = cotangent + jnp.swapaxes(cotangent, 1, 2)
    vec_grad = (jnp.einsum("bij,bje->bie", symmetric, owned_f) / slot_width).astype(jnp.bfloat16)
    vec_grad = vec_grad.reshape(owned_rows, tower_count, -1)
    returned = lax.all_to_all(vec_grad, "tower", split_axis=1, concat_axis=0, tiled=True)
    inverse_own = jnp.argsort(own_row)
    local_grad = returned[:, 0, :][inverse_own]
    gradient = jnp.dot(local_grad, projector[0].T, preferred_element_type=jnp.float32)
    accum = jnp.zeros((row_count, full_width), jnp.float32)
    for depth in reversed(range(depth_count)):
        accum = accum + gradient * scales[depth]
        dscale = (gradient * inputs_f).astype(jnp.bfloat16)
        dhidden = jnp.dot(dscale, whole_up[0, depth], preferred_element_type=jnp.float32).astype(
            jnp.bfloat16
        )
        gradient = gradient + jnp.dot(
            dhidden, whole_down[0, depth].T, preferred_element_type=jnp.float32
        )
    total = (gradient + accum).astype(jnp.bfloat16)
    inverse_place = jnp.argsort(order)
    unplaced = total.reshape(row_count, features, slot_width)[:, inverse_place].reshape(
        1, row_count, full_width
    )
    slab_grad = lax.all_to_all(unplaced, "member", split_axis=2, concat_axis=1, tiled=True)
    return (interactions, slab_grad)


def solution(mesh):
    placed = (
        P("tower", None, "member"),
        P("tower", None, None, "member"),
        P("tower", None, None, "member"),
        P("tower", None, None),
        P("tower", None, None),
        P("tower", None),
        P(),
        P(("tower", "member"), None),
    )
    return jax.shard_map(
        per_device,
        mesh=mesh,
        in_specs=placed,
        out_specs=(P(("tower", "member"), None), P("tower", None, "member")),
        check_vma=False,
    )
```

profile of v0, /device:TPU:2, one launch (start us, length us, event | category | flops | bytes accessed | tf_op | source)
XLA Modules:
  0.0 576.3 jit_solution(18323629134113694175)
XLA Ops:
  7.2 4.7 pad_maximum_fusion
  11.9 6.8 %copy.96 = bf16[1,1024,1024]{2,0,1:T(2,128)(2,1)} copy(bf16[1,1024,1024]{2,1,0:T(8,128)(2,1)} %param.8) | data formatting | bytes 4194304 | tf_op args[0]
  18.7 0.5 broadcast.89
  19.2 14.0 %reduce.1 = bf16[1024,1024]{1,0:T(8,128)(2,1)} reduce(bf16[1024,1,1024]{2,1,0:T(2,128)(2,1)} %bitcast.163, bf16[]{:T(256)} %broadcast.89), dimensions={1}, to_apply=%bitcast.161.reduce_sub_computation | reduce | bytes 4194306
  33.3 4.6 reshape.137
  37.9 5.8 %all-to-all-start = ((bf16[4,2,131072]{2,1,0:T(2,128)(2,1)}), bf16[4,2,131072]{2,1,0:T(2,128)(2,1)}, u32[]{:S(2)}, u32[]{:S(2)}) async-start(bf16[4,2,131072]{2,1,0:T(2,128)(2,1)} %reshape.137), calls=%async_computation | async-start | bytes 4194304 | tf_op jit(solution)/shard_map/all_to_all | solution.py:17
  43.7 0.7 compare_select_fusion
  44.5 104.1 %all-to-all-done = bf16[4,2,131072]{2,1,0:T(2,128)(2,1)} async-done(((bf16[4,2,131072]{2,1,0:T(2,128)(2,1)}), bf16[4,2,131072]{2,1,0:T(2,128)(2,1)}, u32[]{:S(2)}, u32[]{:S(2)}) %all-to-all-start) | async-done | bytes 2097184 | tf_op jit(solution)/shard_map/all_to_all | solution.py:17
  148.6 5.0 reshape.138
  153.5 4.3 copy.52
  157.8 4.0 copy.41
  161.8 4.1 copy.42
  165.9 3.7 gather_fusion
  169.6 183.2 %all-gather.2.cloned.1.call-done = bf16[2,2,4096,512]{3,2,1,0:T(8,128)(2,1)} async-done(((bf16[2,2,4096,128]{3,2,1,0:T(8,128)(2,1)}), bf16[2,2,4096,512]{3,2,1,0:T(8,128)(2,1)}) %all-gather.2.cloned.1.call-update) | async-done | bytes 16777232 | tf_op jit(solution)/shard_map/all_gather | solution.py:9
  352.8 8.4 %convolution_add_fusion.3 = f32[256,4096]{1,0:T(8,128)} fusion(bf16[2,2,4096,512]{3,2,1,0:T(8,128)(2,1)} %all-gather.2.cloned.1.call-done, f32[4096]{0:T(1024)S(1)} %bitcast.179, bf16[32,256,128]{2,1,0:T(8,128)(2,1)} %gather_fusion), kind=kOutput, calls=%fused_computation.12 | convolution fusion | flops 2148663296 | bytes 14696448 | tf_op jit(solution)/shard_map/dot_general | solution.py:39
  361.2 9.6 %convolution_add_fusion.2 = f32[256,4096]{1,0:T(8,128)} fusion(bf16[2,2,4096,512]{3,2,1,0:T(8,128)(2,1)} %all-gather.2.cloned.1.call-done, f32[4096]{0:T(1024)S(1)} %bitcast.178, f32[256,4096]{1,0:T(8,128)} %convolution_add_fusion.3, bf16[32,256,128]{2,1,0:T(8,128)(2,1)} %gather_fusion), kind=kOutput, calls=%fused_computation.11 | convolution fusion | flops 2152857600 | bytes 18890752 | tf_op jit(solution)/shard_map/dot_general | solution.py:39
  370.8 5.0 fusion.41
  375.8 1.2 gather_fusion.1
  377.0 0.6 reduce.2
  377.6 0.7 reshape.139
  378.3 10.3 %all-to-all-start.1 = ((bf16[64,2,512]{2,1,0:T(2,128)(2,1)}), bf16[64,2,512]{2,1,0:T(2,128)(2,1)S(1)}, u32[]{:S(2)}, u32[]{:S(2)}) async-start(bf16[64,2,512]{2,1,0:T(2,128)(2,1)} %reshape.139), calls=%async_computation.1 | async-start | bytes 262144 | tf_op jit(solution)/shard_map/all_to_all | solution.py:47
  388.7 0.1 copy.46
  388.9 3.2 sort.34
  392.0 1.6 sort.35
  393.6 6.5 %all-to-all-done.1 = bf16[64,2,512]{2,1,0:T(2,128)(2,1)S(1)} async-done(((bf16[64,2,512]{2,1,0:T(2,128)(2,1)}), bf16[64,2,512]{2,1,0:T(2,128)(2,1)S(1)}, u32[]{:S(2)}, u32[]{:S(2)}) %all-to-all-start.1) | async-done | bytes 131104 | tf_op jit(solution)/shard_map/all_to_all | solution.py:47
  400.2 0.1 reshape.140
  400.3 0.8 reduce
  401.2 0.2 fusion.40
  401.4 0.8 copy.47
  402.2 6.2 %all-to-all-start.2 = ((bf16[4,64,256]{2,0,1:T(4,128)(2,1)}), bf16[4,64,256]{2,0,1:T(4,128)(2,1)S(1)}, u32[]{:S(2)}, u32[]{:S(2)}) async-start(bf16[4,64,256]{2,0,1:T(4,128)(2,1)} %copy.47), calls=%async_computation.2 | async-start | bytes 262144 | tf_op jit(solution)/shard_map/all_to_all | solution.py:58
  408.4 11.5 %all-to-all-done.2 = bf16[4,64,256]{2,0,1:T(4,128)(2,1)S(1)} async-done(((bf16[4,64,256]{2,0,1:T(4,128)(2,1)}), bf16[4,64,256]{2,0,1:T(4,128)(2,1)S(1)}, u32[]{:S(2)}, u32[]{:S(2)}) %all-to-all-start.2) | async-done | bytes 131104 | tf_op jit(solution)/shard_map/all_to_all | solution.py:58
  419.9 1.2 gather_fusion.2
  421.1 2.7 fusion.19
  423.8 10.9 %convolution_add_fusion.1 = f32[256,4096]{1,0:T(8,128)} fusion(f32[256,4096]{1,0:T(8,128)} %fusion.19, bf16[2,2,4096,512]{3,2,1,0:T(8,128)(2,1)} %all-gather.2.cloned.1.call-done, bf16[32,256,128]{2,1,0:T(8,128)(2,1)} %gather_fusion), kind=kOutput, calls=%fused_computation.10 | convolution fusion | flops 2151809024 | bytes 23068672 | tf_op jit(solution)/shard_map/dot_general | solution.py:69
  434.8 13.5 %fusion.22 = bf16[32,32,8,128]{3,2,1,0:T(8,128)(2,1)} fusion(f32[256,4096]{1,0:T(8,128)} %convolution_add_fusion.1, f32[256,4096]{1,0:T(8,128)} %convolution_add_fusion.3, f32[256,4096]{1,0:T(8,128)} %fusion.19, f32[256,4096]{1,0:T(8,128)} %convolution_add_fusion.2, bf16[2,2,4096,512]{3,2,1,0:T(8,128)(2,1)} %all-gather.2.cloned.1.call-done, ...), kind=kOutput, calls=%fused_computation.38 | convolution fusion | flops 2157051904 | bytes 33554432 | tf_op jit(solution)/shard_map/dot_general | solution.py:69
  448.2 2.2 copy.92
  450.4 2.1 gather_fusion.3
  452.5 3.3 copy.49
  455.8 25.1 %copy.95 = bf16[1,256,4096]{1,0,2:T(2,128)(2,1)} copy(bf16[1,256,4096]{1,2,0:T(8,128)(2,1)S(1)} %bitcast.167) | data formatting | bytes 4194304 | tf_op jit(solution)/shard_map/reshape | solution.py:74
  480.9 21.8 %reduce.3 = bf16[4096,256]{1,0:T(8,128)(2,1)S(1)} reduce(bf16[4096,1,256]{2,1,0:T(2,128)(2,1)} %bitcast.162, bf16[]{:T(256)} %broadcast.89), dimensions={1}, to_apply=%bitcast.160.reduce_sub_computation | reduce | bytes 4194306
  502.6 2.1 reshape.141
  504.7 5.0 all-to-all-start.3
  509.6 0.2 fusion.39
  509.9 0.9 copy.94
  510.7 47.4 %all-to-all-done.3 = bf16[4,2,131072]{2,1,0:T(2,128)(2,1)S(1)} async-done(((bf16[4,2,131072]{2,1,0:T(2,128)(2,1)}), bf16[4,2,131072]{2,1,0:T(2,128)(2,1)S(1)}, u32[]{:S(2)}, u32[]{:S(2)}) %all-to-all-start.3) | async-done | bytes 2097184 | tf_op jit(solution)/shard_map/all_to_all | solution.py:77
  558.1 3.4 reshape.142
  561.5 4.0 copy.54
  565.5 3.9 copy.51
  (31 shorter events, 0.4 us)
Async XLA Ops:
  7.2 363.6 %copy-start = (bf16[1,4096,256]{2,1,0:T(8,128)(2,1)S(1)}, bf16[1,4096,256]{2,1,0:T(8,128)(2,1)}, u32[]{:S(2)}) copy-start(bf16[1,4096,256]{2,1,0:T(8,128)(2,1)} %param.12) | copy-start | bytes 6291460
  7.2 345.6 %all-gather.2.cloned.1.call-start = ((), (), s32[]{:S(2)}) async-start(), calls=%async_computation.4 | async-start | bytes 20971520 | tf_op jit(solution)/shard_map/all_gather | solution.py:9
  33.3 11.1 %copy-start.5 = (s32[1,32]{1,0:T(1,128)S(1)}, s32[1,32]{1,0:T(1,128)}, u32[]{:S(2)}) copy-start(s32[1,32]{1,0:T(1,128)} %param.13) | copy-start | bytes 388
  33.3 11.2 %copy-start.4 = (f32[1,2,4096]{2,1,0:T(2,128)S(1)}, f32[1,2,4096]{2,1,0:T(2,128)}, u32[]{:S(2)}) copy-start(f32[1,2,4096]{2,1,0:T(2,128)} %param.11) | copy-start | bytes 98308
  37.9 110.7 %all-to-all-start = ((bf16[4,2,131072]{2,1,0:T(2,128)(2,1)}), bf16[4,2,131072]{2,1,0:T(2,128)(2,1)}, u32[]{:S(2)}, u32[]{:S(2)}) async-start(bf16[4,2,131072]{2,1,0:T(2,128)(2,1)} %reshape.137), calls=%async_computation | async-start | bytes 4194304 | tf_op jit(solution)/shard_map/all_to_all | solution.py:17
  370.8 17.8 %copy-start.3 = (bf16[4,16384]{1,0:T(4,128)(2,1)S(1)}, bf16[4,16384]{1,0:T(4,128)(2,1)}, u32[]{:S(2)}) copy-start(bf16[4,16384]{1,0:T(4,128)(2,1)} %param.15) | copy-start | bytes 393220
  378.3 21.8 %all-to-all-start.1 = ((bf16[64,2,512]{2,1,0:T(2,128)(2,1)}), bf16[64,2,512]{2,1,0:T(2,128)(2,1)S(1)}, u32[]{:S(2)}, u32[]{:S(2)}) async-start(bf16[64,2,512]{2,1,0:T(2,128)(2,1)} %reshape.139), calls=%async_computation.1 | async-start | bytes 262144 | tf_op jit(solution)/shard_map/all_to_all | solution.py:47
  402.2 17.7 %all-to-all-start.2 = ((bf16[4,64,256]{2,0,1:T(4,128)(2,1)}), bf16[4,64,256]{2,0,1:T(4,128)(2,1)S(1)}, u32[]{:S(2)}, u32[]{:S(2)}) async-start(bf16[4,64,256]{2,0,1:T(4,128)(2,1)} %copy.47), calls=%async_computation.2 | async-start | bytes 262144 | tf_op jit(solution)/shard_map/all_to_all | solution.py:58
  423.8 11.0 %copy-start.2 = (bf16[32,256,128]{2,1,0:T(8,128)(2,1)S(1)}, bf16[32,256,128]{2,1,0:T(8,128)(2,1)}, u32[]{:S(2)}) copy-start(bf16[32,256,128]{2,1,0:T(8,128)(2,1)} %gather_fusion) | copy-start | bytes 6291460
  504.7 53.4 %all-to-all-start.3 = ((bf16[4,2,131072]{2,1,0:T(2,128)(2,1)}), bf16[4,2,131072]{2,1,0:T(2,128)(2,1)S(1)}, u32[]{:S(2)}, u32[]{:S(2)}) async-start(bf16[4,2,131072]{2,1,0:T(2,128)(2,1)} %reshape.141), calls=%async_computation.3 | async-start | bytes 4194304 | tf_op jit(solution)/shard_map/all_to_all | solution.py:77
  561.5 8.0 %copy-start.1 = (bf16[1,4096,256]{2,1,0:T(8,128)(2,1)S(1)}, bf16[1,4096,256]{2,1,0:T(8,128)(2,1)}, u32[]{:S(2)}) copy-start(bf16[1,4096,256]{2,1,0:T(8,128)(2,1)} %param.12) | copy-start | bytes 6291460
Sparse Core Ops, SparseCore 0:
  12.0 340.6 all-gather.1
where the time goes:
time: 578 us; the launch traced here: 576 us
  waiting for transfers between devices  353 us (61%)
  local copies, waits for them, and re-layouts  84.1 us (15%)
  matrix products  50.5 us (9%)
  other arithmetic  47.4 us (8%)
  starting transfers between devices  27.4 us (5%)
  between operations  14.3 us (2%)
    all_gather x1, waiting for transfers between devices, side_by_side(): lax.all_gather(both, axis, axis=dim, tiled=True)  183 us
    all_to_all x1, waiting for transfers between devices, per_device(): lax.all_to_all(slabs, 'member', split_axis=1, concat_axis=2, tiled=True)  104 us
    all_to_all x1, waiting for transfers between devices, per_device(): lax.all_to_all(unplaced, 'member', split_axis=2, concat_axis=1, tiled=True)  47.4 us
    unnamed x3, other arithmetic  35.8 us
    unnamed x24, local copies, waits for them, and re-layouts  32.4 us
    reshape x2, local copies, waits for them, and re-layouts, per_device(): total.reshape(row_count, features, slot_width)[:, inverse_place]  27.2 us
    dot_general x2, matrix products, per_device(): jnp.dot(dhidden, whole_down[0, depth].T, preferred_element_type=jnp.float32)  24.4 us
    dot_general x2, matrix products, per_device(): jnp.dot(hidden, whole_up[0, depth].T, preferred_element_type=jnp.float32)  18.1 us
  transfers between devices with their start and end apart: 5, of which 5 were waited for; matrix products, arithmetic and copies ran while one was open for 9% of the time, Pallas kernels for 0%

commit v1 on v0

v1 whole, which is shorter than its diff:
```python
import functools

import jax
import jax.numpy as jnp
from jax import lax
from jax.experimental import pallas as pl
from jax.experimental.pallas import tpu as pltpu
from jax.sharding import PartitionSpec as P

F32 = jnp.float32
BF16 = jnp.bfloat16
E = 128
N = 4
NB = 256
NT = (((1,), (1,)), ((), ()))


def dot(a, b):
    return jnp.dot(a, b, preferred_element_type=F32)


def dot_t(a, b):
    return lax.dot_general(a, b, NT, preferred_element_type=F32)


def line_position():
    me = lax.axis_index("member")
    near = me + 1 - 2 * (me % 2)
    hub = ((me + 1) // 2) % 2
    return me, near, 3 - me, hub


def greet(me):
    barrier = pltpu.get_barrier_semaphore()
    for d in range(1, N):
        pl.semaphore_signal(barrier, inc=1, device_id={"member": (me + d) % N})
    pl.semaphore_wait(barrier, N - 1)


class LineSum:
    def __init__(self, block, total, own, part, from_end, side, from_side, sems):
        self.me, self.near, self.across, self.hub = line_position()
        self.block, self.total, self.own = block, total, own
        self.part, self.from_end, self.side, self.from_side = part, from_end, side, from_side
        self.sems = sems

    def rows(self, c):
        return pl.ds(pl.multiple_of(c * self.block, self.block), self.block)

    def copy(self, kind, src, dst, layer, c, peer):
        rows = self.rows(c)
        return pltpu.make_async_remote_copy(
            src_ref=src.at[layer, rows],
            dst_ref=dst.at[layer, rows],
            send_sem=self.sems.at[2 * kind, layer, c],
            recv_sem=self.sems.at[2 * kind + 1, layer, c],
            device_id={"member": peer},
        )

    def to_hub(self, layer, c):
        return self.copy(0, self.part, self.from_end, layer, c, self.near)

    def to_side(self, layer, c):
        return self.copy(1, self.side, self.from_side, layer, c, self.across)

    def to_end(self, layer, c):
        return self.copy(2, self.total, self.total, layer, c, self.near)

    def put(self, layer, c, value):
        @pl.when(self.hub == 1)
        def _():
            self.own[self.rows(c), :] = value

        @pl.when(self.hub == 0)
        def _():
            self.part[layer, self.rows(c), :] = value.astype(BF16)
            self.to_hub(layer, c).start()

    def exchange(self, layer, c):
        rows = self.rows(c)

        @pl.when(self.hub == 1)
        def _():
            self.to_hub(layer, c).wait_recv()
            both = self.own[rows, :] + self.from_end[layer, rows, :].astype(F32)
            self.side[layer, rows, :] = both.astype(BF16)
            self.to_side(layer, c).start()

    def get(self, layer, c):
        rows = self.rows(c)

        @pl.when(self.hub == 1)
        def _():
            self.to_side(layer, c).wait_recv()
            whole = self.side[layer, rows, :].astype(F32) + self.from_side[layer, rows, :].astype(F32)
            self.total[layer, rows, :] = whole.astype(BF16)
            self.to_end(layer, c).start()

        @pl.when(self.hub == 0)
        def _():
            self.to_end(layer, c).wait_recv()

    def drain(self, layer, c):
        @pl.when(self.hub == 1)
        def _():
            self.to_side(layer, c).wait_send()
            self.to_end(layer, c).wait_send()

        @pl.when(self.hub == 0)
        def _():
            self.to_hub(layer, c).wait_send()


def each(count, body):
    lax.fori_loop(0, count, lambda i, _: (body(i), 0)[1], 0)


def ranks(w_ref, k, lo, rows):
    return jnp.concatenate([w_ref[k, r, lo : lo + rows, :] for r in range(N)], axis=1)


def times_down(a, w_ref, k):
    width = w_ref.shape[2]
    halves = []
    for j in range(0, N, 2):
        right = jnp.concatenate([w_ref[k, j], w_ref[k, j + 1]], axis=1)
        halves.append(dot(a, right))
    return jnp.concatenate(halves, axis=1)


def forward_kernel(
    inv_ref, own_ref, x_ref, down_ref, up_ref, bias_ref, proj_ref,
    ordered_ref, w_ref, pw_ref, h_ref, bw_ref,
    stage, cur, own, part, from_end, side, from_side, v_out, v_own, v_in,
    sems, w_sems, v_sems,
):
    samples, width = x_ref.shape
    block = samples // N
    line = LineSum(block, h_ref, own, part, from_end, side, from_side, sems)
    me = line.me
    feats = width // E

    def send_w(k, d):
        peer = (me + d) % N
        return pltpu.make_async_remote_copy(
            src_ref=stage.at[k, peer],
            dst_ref=w_ref.at[k, me],
            send_sem=w_sems.at[0, k, peer],
            recv_sem=w_sems.at[1, k, me],
            device_id={"member": peer},
        )

    def recv_w(k, d):
        peer = (me + d) % N
        return pltpu.make_async_remote_copy(
            src_ref=stage.at[k, peer],
            dst_ref=w_ref.at[k, peer],
            send_sem=w_sems.at[0, k, peer],
            recv_sem=w_sems.at[1, k, peer],
            device_id={"member": peer},
        )

    def stage_w(k):
        source = down_ref if k % 2 == 0 else up_ref

        def one(f):
            at = pl.multiple_of((f % feats) * E, E)
            stage[k, f // feats, pl.ds(at, E), :] = source[k // 2, inv_ref[f]]

        each(N * feats, one)
        w_ref[k, me] = stage[k, me]

    def start_w(k):
        for d in range(1, N):
            send_w(k, d).start()

    def sent_w(k):
        for d in range(1, N):
            send_w(k, d).wait_send()

    def got_w(k):
        for d in range(1, N):
            recv_w(k, d).wait_recv()

    greet(me)
    stage_w(0)
    start_w(0)
    for k in range(1, 4):
        stage_w(k)
    for i in range(feats):
        slot = inv_ref[me * feats + i]
        pw_ref[i * E : (i + 1) * E, :] = proj_ref[slot]
        for layer in range(2):
            bw_ref[layer, :, i * E : (i + 1) * E] = bias_ref[layer, slot]
    sent_w(0)
    start_w(1)
    got_w(0)
    each(N, lambda c: line.put(0, c, times_down(x_ref[line.rows(c), :], w_ref, 0)))
    each(N, lambda c: line.exchange(0, c))
    sent_w(1)
    start_w(2)
    each(N, lambda c: line.get(0, c))
    got_w(1)

    def next_current(layer, c):
        rows = line.rows(c)
        hidden = h_ref[layer, rows, :]
        for lo in range(0, width, NB):
            cols = slice(lo, lo + NB)
            scale = dot_t(hidden, ranks(w_ref, 2 * layer + 1, lo, NB)) + bw_ref[layer, :, cols]
            x = x_ref[rows, cols].astype(F32)
            before = x if layer == 0 else cur[rows, cols].astype(F32)
            cur[rows, cols] = (x * scale + before).astype(BF16)

    each(N, lambda c: next_current(0, c))
    sent_w(2)
    start_w(3)
    got_w(2)
    each(N, lambda c: line.put(1, c, times_down(cur[line.rows(c), :], w_ref, 2)))
    each(N, lambda c: line.exchange(1, c))
    each(N, lambda c: line.get(1, c))
    got_w(3)

    def v_copy(slot, peer):
        return pltpu.make_async_remote_copy(
            src_ref=v_out.at[peer],
            dst_ref=v_in.at[slot],
            send_sem=v_sems.at[0, peer],
            recv_sem=v_sems.at[1, slot],
            device_id={"member": peer},
        )

    def vectors(c):
        next_current(1, c)
        part_v = dot(cur[line.rows(c), :], pw_ref[...])

        @pl.when(c == me)
        def _():
            v_own[...] = part_v

        @pl.when(c != me)
        def _():
            v_out[c] = part_v.astype(BF16)
            v_copy(me, c).start()

    each(N, vectors)
    vector = v_own[...]
    for d in range(1, N):
        peer = (me + d) % N
        v_copy(peer, peer).wait_recv()
        vector = vector + v_in[peer].astype(F32)
    vector = vector.astype(BF16)
    shape = (2 * block, block)
    hit = own_ref[...] == lax.broadcasted_iota(jnp.int32, shape, 1)
    odd = lax.broadcasted_iota(jnp.int32, shape, 0) % 2
    total = jnp.zeros((2 * block, E), F32)
    for k in range(2):
        pick = jnp.where(hit & (odd == k), 1.0, 0.0).astype(BF16)
        total = total + dot(pick, vector[:, k * E : (k + 1) * E])
    ordered_ref[...] = total.astype(BF16)

    sent_w(3)
    for d in range(1, N):
        v_copy(me, (me + d) % N).wait_send()
    for layer in range(2):
        each(N, lambda c: line.drain(layer, c))


def backward_kernel(
    own_ref, ret_ref, x_ref, w_ref, pw_ref, h_ref, bw_ref,
    out_ref,
    vg, grad, scales, own, part, from_end, side, from_side, dh,
    sems, v_sems,
):
    samples, width = x_ref.shape
    block = samples // N
    line = LineSum(block, dh, own, part, from_end, side, from_side, sems)
    me = line.me
    greet(me)

    shape = (block, 2 * block)
    hit = own_ref[...] == lax.broadcasted_iota(jnp.int32, shape, 0)
    odd = lax.broadcasted_iota(jnp.int32, shape, 1) % 2
    for k in range(2):
        pick = jnp.where(hit & (odd == k), 1.0, 0.0).astype(BF16)
        vg[me, :, k * E : (k + 1) * E] = dot(pick, ret_ref[...]).astype(BF16)

    def v_copy(slot, peer):
        return pltpu.make_async_remote_copy(
            src_ref=vg.at[slot],
            dst_ref=vg.at[slot],
            send_sem=v_sems.at[0, peer],
            recv_sem=v_sems.at[1, slot],
            device_id={"member": peer},
        )

    for d in range(1, N):
        v_copy(me, (me + d) % N).start()

    def scale_of(c):
        rows = line.rows(c)
        for layer in range(2):
            hidden = h_ref[layer, rows, :]
            for lo in range(0, width, NB):
                cols = slice(lo, lo + NB)
                scale = dot_t(hidden, ranks(w_ref, 2 * layer + 1, lo, NB)) + bw_ref[layer, :, cols]
                scales[layer, rows, cols] = scale

    each(N, scale_of)
    for d in range(1, N):
        v_copy((me + d) % N, (me + d) % N).wait_recv()

    def last_layer(c):
        rows = line.rows(c)
        total = jnp.zeros((block, w_ref.shape[1] * w_ref.shape[3]), F32)
        for lo in range(0, width, NB):
            cols = slice(lo, lo + NB)
            g = dot_t(vg[c], pw_ref[cols, :])
            grad[rows, cols] = g
            dscale = (g * x_ref[rows, cols].astype(F32)).astype(BF16)
            total = total + dot(dscale, ranks(w_ref, 3, lo, NB))
        line.put(0, c, total)

    each(N, last_layer)
    each(N, lambda c: line.exchange(0, c))

    def first_layer(c):
        rows = line.rows(c)
        line.get(0, c)
        dhidden = dh[0, rows, :]
        total = jnp.zeros((block, w_ref.shape[1] * w_ref.shape[3]), F32)
        for lo in range(0, width, NB):
            cols = slice(lo, lo + NB)
            g2 = grad[rows, cols]
            g1 = g2 + dot_t(dhidden, ranks(w_ref, 2, lo, NB))
            grad[rows, cols] = g1 + (g2 * scales[1, rows, cols] + g1 * scales[0, rows, cols])
            dscale = (g1 * x_ref[rows, cols].astype(F32)).astype(BF16)
            total = total + dot(dscale, ranks(w_ref, 1, lo, NB))
        line.put(1, c, total)

    each(N, first_layer)
    each(N, lambda c: line.exchange(1, c))

    def finish(c):
        rows = line.rows(c)
        line.get(1, c)
        dhidden = dh[1, rows, :]
        for lo in range(0, width, NB):
            cols = slice(lo, lo + NB)
            g0 = grad[rows, cols] + dot_t(dhidden, ranks(w_ref, 0, lo, NB))
            out_ref[rows, cols] = g0.astype(BF16)

    each(N, finish)
    for d in range(1, N):
        v_copy(me, (me + d) % N).wait_send()
    for layer in range(2):
        each(N, lambda c: line.drain(layer, c))


def line_scratch(samples, rank):
    return [pltpu.VMEM((samples, rank), F32)] + [pltpu.VMEM((2, samples, rank), BF16)] * 4


def vmem():
    return pl.BlockSpec(memory_space=pltpu.VMEM)


def params(collective_id):
    return pltpu.CompilerParams(
        collective_id=collective_id, has_side_effects=True, vmem_limit_bytes=60 << 20
    )


def per_device(slabs, cross_down, cross_up, cross_bias, projector, placement, owner, inter_grad):
    x = slabs[0]
    samples, width = x.shape
    block = samples // N
    slots = placement.shape[1]
    rank = N * cross_down.shape[3]
    towers = block // 4
    order = placement[0]
    index = jnp.arange(slots, dtype=jnp.int32)
    inverse = jnp.sum(jnp.where(order[None, :] == index[:, None], index[None, :], 0), axis=1)
    own_row = lax.dynamic_index_in_dim(owner, lax.axis_index("member"), 0, keepdims=False)
    own_twice = jnp.repeat(own_row, 2)
    sds = jax.ShapeDtypeStruct
    ordered, w, pw, hidden, bw = pl.pallas_call(
        forward_kernel,
        out_shape=(
            sds((2 * block, E), BF16),
            sds((4, N, width, E), BF16),
            sds((width, 2 * E), BF16),
            sds((2, samples, rank), BF16),
            sds((2, 1, width), F32),
        ),
        in_specs=[pl.BlockSpec(memory_space=pltpu.SMEM)] + [vmem()] * 6,
        out_specs=(vmem(),) * 5,
        scratch_shapes=[
            pltpu.VMEM((4, N, width, E), BF16),
            pltpu.VMEM((samples, width), BF16),
            *line_scratch(samples, rank),
            pltpu.VMEM((N, block, 2 * E), BF16),
            pltpu.VMEM((block, 2 * E), F32),
            pltpu.VMEM((N, block, 2 * E), BF16),
            pltpu.SemaphoreType.DMA((6, 2, N)),
            pltpu.SemaphoreType.DMA((2, 4, N)),
            pltpu.SemaphoreType.DMA((2, N)),
        ],
        compiler_params=params(0),
        name="forward",
    )(
        inverse, own_twice[:, None], x,
        cross_down[0].reshape(2, slots, E, E), cross_up[0].reshape(2, slots, E, E),
        cross_bias[0].reshape(2, slots, 1, E), projector[0].reshape(slots, E, 2 * E),
    )

    owned = lax.all_to_all(ordered.reshape(towers, 8, E), "tower", split_axis=0, concat_axis=0, tiled=True)
    vectors = owned.reshape(towers, 4, 2, E).transpose(1, 0, 2, 3).reshape(4, 2 * towers, E)
    table = jnp.einsum("bie,bje->bij", vectors, vectors, preferred_element_type=F32) / E
    interactions = table.reshape(4, -1)
    cot = inter_grad.astype(F32).reshape(4, 2 * towers, 2 * towers)
    symmetric = cot + jnp.swapaxes(cot, 1, 2)
    vec_grad = (jnp.einsum("bij,bje->bie", symmetric, vectors.astype(F32)) / E).astype(BF16)
    back = vec_grad.reshape(4, towers, 2, E).transpose(1, 0, 2, 3).reshape(towers, 8, E)
    returned = lax.all_to_all(back, "tower", split_axis=0, concat_axis=0, tiled=True)

    slab_grad = pl.pallas_call(
        backward_kernel,
        out_shape=sds((samples, width), BF16),
        in_specs=[vmem()] * 7,
        out_specs=vmem(),
        scratch_shapes=[
            pltpu.VMEM((N, block, 2 * E), BF16),
            pltpu.VMEM((samples, width), F32),
            pltpu.VMEM((2, samples, width), F32),
            *line_scratch(samples, rank),
            pltpu.VMEM((2, samples, rank), BF16),
            pltpu.SemaphoreType.DMA((6, 2, N)),
            pltpu.SemaphoreType.DMA((2, N)),
        ],
        compiler_params=params(1),
        name="backward",
    )(own_twice[None, :], returned.reshape(2 * block, E), x, w, pw, hidden, bw)
    return interactions, slab_grad[None]


def solution(mesh):
    placed = (
        P("tower", None, "member"),
        P("tower", None, None, "member"),
        P("tower", None, None, "member"),
        P("tower", None, None),
        P("tower", None, None),
        P("tower", None),
        P(),
        P(("tower", "member"), None),
    )
    return jax.shard_map(
        per_device,
        mesh=mesh,
        in_specs=placed,
        out_specs=(P(("tower", "member"), None), P("tower", None, "member")),
        check_vma=False,
    )
```

time: 578 us -> 346 us (0.60)
  waiting for transfers between devices: 353 us -> 21.1 us
  Pallas kernels: 0 us -> 297 us
  local copies, waits for them, and re-layouts: 84.1 us -> 8.62 us
  matrix products: 50.5 us -> 0.38 us
  other arithmetic: 47.4 us -> 1.39 us
  between operations: 14.3 us -> 0.74 us
  starting transfers between devices: 27.4 us -> 16.1 us
    pallas_call x0 -> x2, Pallas kernels: none -> 297 us  [the longest x1 196 us: per_device(): pl.pallas_call(forward_kernel, out_shape=(sds((2 * block, E), BF16), sds(...]
    all_gather x1 -> x0, waiting for transfers between devices: 183 us -> none  [side_by_side(): lax.all_gather(both, axis, axis=dim, tiled=True)]
    all_to_all x4 -> x2, waiting for transfers between devices: 169 us -> 21.1 us  [the longest x1 11.3 us: per_device(): lax.all_to_all(ordered.reshape(towers, 8, E), 'tower', split_axis=0, conc...]
    dot_general x8 -> x2, matrix products: 50.5 us -> 0.38 us  [the longest x1 0.2 us: per_device(): jnp.einsum('bie,bje->bij', vectors, vectors, preferred_element_type=F32) / E]
    unnamed x3 -> x1, other arithmetic: 35.8 us -> 0.03 us
    reshape x6 -> x2, local copies, waits for them, and re-layouts: 28.2 us -> 0.22 us  [the longest x1 0.13 us: per_device(): cot = inter_grad.astype(F32).reshape(4, 2 * towers, 2 * towers)]
    unnamed x24 -> x9, local copies, waits for them, and re-layouts: 32.4 us -> 4.64 us
    gather x5 -> x0, local copies, waits for them, and re-layouts: 11.4 us -> none  [the longest x2 5.4 us: per_device(): total.reshape(row_count, features, slot_width)[:, inverse_place]]
  transfers between devices with their start and end apart: 5 -> 2, of which waited for: 5 -> 2; matrix products, arithmetic and copies ran while one was open for 9% -> 1% of each run, Pallas kernels for 0% -> 0%
where the time goes in v1:
time: 346 us; the launch traced here: 345 us
  Pallas kernels  297 us (86%)
  waiting for transfers between devices  21.1 us (6%)
  starting transfers between devices  16.1 us (5%)
  local copies, waits for them, and re-layouts  8.62 us (2%)
    pallas_call x1, Pallas kernels, per_device(): pl.pallas_call(forward_kernel, out_shape=(sds((2 * block, E), BF16), sds(...  196 us
    pallas_call x1, Pallas kernels, per_device(): pl.pallas_call(backward_kernel, out_shape=sds((samples, width), BF16), in...  101 us
    all_to_all x1, waiting for transfers between devices, per_device(): lax.all_to_all(ordered.reshape(towers, 8, E), 'tower', split_axis=0, conc...  11.3 us
    all_to_all x1, starting transfers between devices, per_device(): lax.all_to_all(ordered.reshape(towers, 8, E), 'tower', split_axis=0, conc...  10.4 us
    all_to_all x1, waiting for transfers between devices, per_device(): lax.all_to_all(back, 'tower', split_axis=0, concat_axis=0, tiled=True)  9.71 us
  transfers between devices with their start and end apart: 2, of which 2 were waited for; matrix products, arithmetic and copies ran while one was open for 1% of the time, Pallas kernels for 0%

profile of v1, /device:TPU:2, one launch (start us, length us, event | category | flops | bytes accessed | tf_op | source)
XLA Modules:
  0.0 345.3 jit_solution(256186894445658267)
XLA Ops:
  0.6 0.0 copy-start
  0.6 1.4 select_reduce_fusion.inv_ref
  2.0 1.4 reshape_squeeze.14.bias_ref
  3.4 0.0 copy-done
  3.4 0.1 broadcast_in_dim.22
  3.5 0.8 broadcast_in_dim_reshape.8.own_ref
  4.4 0.0 copy-start.2
  4.4 195.8 %forward.1 = (bf16[512,128]{1,0:T(8,128)(2,1)}, bf16[4,4,1024,128]{3,2,1,0:T(8,128)(2,1)}, bf16[1024,256]{1,0:T(8,128)(2,1)}, bf16[2,1024,512]{2,1,0:T(8,128)(2,1)}, f32[2,1,1024]{2,1,0:T(1,128)}) custom-call(s32[32]{0:T(128)} %select_reduce_fusion.inv_ref, s32[512,1]{1,0:T(8,128)} %broadcast_in_dim_reshape.8.own_ref, bf16[1024,1024]{1,0:T(8,128)(2,1)} %bitcast.36, ...), custom_call_target="tpu_custom_call" | custom-call | tf_op jit(solution)/shard_map/forward/pallas_call | solution.py:387
  200.2 10.4 %all-to-all-start = ((bf16[64,8,128]{2,1,0:T(8,128)(2,1)}), bf16[64,8,128]{2,1,0:T(8,128)(2,1)S(1)}, u32[]{:S(2)}, u32[]{:S(2)}) async-start(bf16[64,8,128]{2,1,0:T(8,128)(2,1)} %bitcast.49), calls=%async_computation | async-start | bytes 262144 | tf_op jit(solution)/shard_map/all_to_all | solution.py:417
  210.6 0.0 copy-done.2
  210.7 0.1 copy.19
  210.8 11.3 %all-to-all-done = bf16[64,8,128]{2,1,0:T(8,128)(2,1)S(1)} async-done(((bf16[64,8,128]{2,1,0:T(8,128)(2,1)}), bf16[64,8,128]{2,1,0:T(8,128)(2,1)S(1)}, u32[]{:S(2)}, u32[]{:S(2)}) %all-to-all-start) | async-done | bytes 131104 | tf_op jit(solution)/shard_map/all_to_all | solution.py:417
  222.1 0.1 copy.18
  222.2 0.2 fusion.1
  222.4 0.7 copy.20
  223.2 5.6 %all-to-all-start.1 = ((bf16[64,8,128]{2,1,0:T(8,128)(2,1)}), bf16[64,8,128]{2,1,0:T(8,128)(2,1)S(1)}, u32[]{:S(2)}, u32[]{:S(2)}) async-start(bf16[64,8,128]{2,1,0:T(8,128)(2,1)} %bitcast.14), calls=%async_computation.1 | async-start | bytes 262144 | tf_op jit(solution)/shard_map/all_to_all | solution.py:425
  228.8 0.7 broadcast_in_dim_reshape.7.own_ref
  229.5 0.2 fusion
  229.7 0.9 copy.29
  230.6 9.7 %all-to-all-done.1 = bf16[64,8,128]{2,1,0:T(8,128)(2,1)S(1)} async-done(((bf16[64,8,128]{2,1,0:T(8,128)(2,1)}), bf16[64,8,128]{2,1,0:T(8,128)(2,1)S(1)}, u32[]{:S(2)}, u32[]{:S(2)}) %all-to-all-start.1) | async-done | bytes 131104 | tf_op jit(solution)/shard_map/all_to_all | solution.py:425
  240.3 0.0 copy-start.1
  240.3 0.7 copy-done.1
  240.9 101.2 %backward.1 = bf16[1024,1024]{1,0:T(8,128)(2,1)} custom-call(s32[1,512]{1,0:T(1,128)} %broadcast_in_dim_reshape.7.own_ref, bf16[512,128]{1,0:T(8,128)(2,1)} %bitcast.45, bf16[1024,1024]{1,0:T(8,128)(2,1)} %bitcast.37, bf16[4,4,1024,128]{3,2,1,0:T(8,128)(2,1)} %get-tuple-element.8.w_ref, bf16[1024,256]{1,0:T(8,128)(2,1)} %get-tuple-element.9.pw_ref, ...), custom_call_target="tpu_custom_call" | custom-call | tf_op jit(solution)/shard_map/backward/pallas_call | solution.py:427
  342.2 3.1 copy.31
  (3 shorter events, 0.1 us)
Async XLA Ops:
  0.6 2.8 copy-start
  4.4 206.2 %copy-start.2 = (bf16[4,16384]{1,0:T(4,128)(2,1)S(1)}, bf16[4,16384]{1,0:T(4,128)(2,1)}, u32[]{:S(2)}) copy-start(bf16[4,16384]{1,0:T(4,128)(2,1)} %param.15) | copy-start | bytes 393220
  200.2 22.0 %all-to-all-start = ((bf16[64,8,128]{2,1,0:T(8,128)(2,1)}), bf16[64,8,128]{2,1,0:T(8,128)(2,1)S(1)}, u32[]{:S(2)}, u32[]{:S(2)}) async-start(bf16[64,8,128]{2,1,0:T(8,128)(2,1)} %bitcast.49), calls=%async_computation | async-start | bytes 262144 | tf_op jit(solution)/shard_map/all_to_all | solution.py:417
  223.2 17.1 %all-to-all-start.1 = ((bf16[64,8,128]{2,1,0:T(8,128)(2,1)}), bf16[64,8,128]{2,1,0:T(8,128)(2,1)S(1)}, u32[]{:S(2)}, u32[]{:S(2)}) async-start(bf16[64,8,128]{2,1,0:T(8,128)(2,1)} %bitcast.14), calls=%async_computation.1 | async-start | bytes 262144 | tf_op jit(solution)/shard_map/all_to_all | solution.py:425
  240.3 0.7 copy-start.1

commit v2 on v1

--- a/solution.py
+++ b/solution.py
@@ -13,6 +13,7 @@
 N = 4
 NB = 256
 NT = (((1,), (1,)), ((), ()))
+TN = (((0,), (0,)), ((), ()))
 
 
 def dot(a, b):
@@ -74,6 +75,11 @@
         @pl.when(self.hub == 0)
         def _():
             self.part[layer, self.rows(c), :] = value.astype(BF16)
+
+            @pl.when(c > 0)
+            def _():
+                self.to_hub(layer, c - 1).wait_send()
+
             self.to_hub(layer, c).start()
 
     def exchange(self, layer, c):
@@ -100,19 +106,31 @@
         def _():
             self.to_end(layer, c).wait_recv()
 
-    def drain(self, layer, c):
+    def lag(self, hub, end):
+        return hub * self.hub + end * (1 - self.hub)
+
+    def drain(self, layer):
         @pl.when(self.hub == 1)
         def _():
-            self.to_side(layer, c).wait_send()
-            self.to_end(layer, c).wait_send()
+            def both(c):
+                self.to_side(layer, c).wait_send()
+                self.to_end(layer, c).wait_send()
+
+            each(N, both)
 
         @pl.when(self.hub == 0)
         def _():
-            self.to_hub(layer, c).wait_send()
+            self.to_hub(layer, N - 1).wait_send()
 
 
 def each(count, body):
     lax.fori_loop(0, count, lambda i, _: (body(i), 0)[1], 0)
+
+
+def stage(c, body):
+    @pl.when((c >= 0) & (c < N))
+    def _():
+        body(c)
 
 
 def ranks(w_ref, k, lo, rows):
@@ -131,7 +149,7 @@
 def forward_kernel(
     inv_ref, own_ref, x_ref, down_ref, up_ref, bias_ref, proj_ref,
     ordered_ref, w_ref, pw_ref, h_ref, bw_ref,
-    stage, cur, own, part, from_end, side, from_side, v_out, v_own, v_in,
+    ready, cur, own, part, from_end, side, from_side, v_out, v_own, v_in,
     sems, w_sems, v_sems,
 ):
     samples, width = x_ref.shape
@@ -143,7 +161,7 @@
     def send_w(k, d):
         peer = (me + d) % N
         return pltpu.make_async_remote_copy(
-            src_ref=stage.at[k, peer],
+            src_ref=ready.at[k, peer],
             dst_ref=w_ref.at[k, me],
             send_sem=w_sems.at[0, k, peer],
             recv_sem=w_sems.at[1, k, me],
@@ -153,7 +171,7 @@
     def recv_w(k, d):
         peer = (me + d) % N
         return pltpu.make_async_remote_copy(
-            src_ref=stage.at[k, peer],
+            src_ref=ready.at[k, peer],
             dst_ref=w_ref.at[k, peer],
             send_sem=w_sems.at[0, k, peer],
             recv_sem=w_sems.at[1, k, peer],
@@ -165,26 +183,28 @@
 
         def one(f):
             at = pl.multiple_of((f % feats) * E, E)
-            stage[k, f // feats, pl.ds(at, E), :] = source[k // 2, inv_ref[f]]
+            ready[k, f // feats, pl.ds(at, E), :] = source[k // 2, inv_ref[f]]
 
         each(N * feats, one)
-        w_ref[k, me] = stage[k, me]
-
-    def start_w(k):
-        for d in range(1, N):
-            send_w(k, d).start()
-
-    def sent_w(k):
-        for d in range(1, N):
-            send_w(k, d).wait_send()
+        w_ref[k, me] = ready[k, me]
 
     def got_w(k):
         for d in range(1, N):
             recv_w(k, d).wait_recv()
 
+    def pump(j):
+        @pl.when((j > 0) & (j < 9))
+        def _():
+            send_w(1 + (j - 1) // 3, 1 + (j - 1) % 3).wait_send()
+
+        @pl.when(j < 9)
+        def _():
+            send_w(1 + j // 3, 1 + j % 3).start()
+
     greet(me)
     stage_w(0)
-    start_w(0)
+    for d in range(1, N):
+        send_w(0, d).start()
     for k in range(1, 4):
         stage_w(k)
     for i in range(feats):
@@ -192,15 +212,19 @@
         pw_ref[i * E : (i + 1) * E, :] = proj_ref[slot]
         for layer in range(2):
             bw_ref[layer, :, i * E : (i + 1) * E] = bias_ref[layer, slot]
-    sent_w(0)
-    start_w(1)
+    for d in range(1, N):
+        send_w(0, d).wait_send()
     got_w(0)
-    each(N, lambda c: line.put(0, c, times_down(x_ref[line.rows(c), :], w_ref, 0)))
-    each(N, lambda c: line.exchange(0, c))
-    sent_w(1)
-    start_w(2)
-    each(N, lambda c: line.get(0, c))
+
+    def first_sum(i):
+        pump(i)
+        stage(i, lambda c: line.put(0, c, times_down(x_ref[line.rows(c), :], w_ref, 0)))
+        stage(i, lambda c: line.exchange(0, c))
+        stage(i - line.lag(1, 3), lambda c: line.get(0, c))
+
+    each(N + 3, first_sum)
     got_w(1)
+    got_w(2)
 
     def next_current(layer, c):
         rows = line.rows(c)
@@ -212,15 +236,6 @@
             before = x if layer == 0 else cur[rows, cols].astype(F32)
             cur[rows, cols] = (x * scale + before).astype(BF16)
 
-    each(N, lambda c: next_current(0, c))
-    sent_w(2)
-    start_w(3)
-    got_w(2)
-    each(N, lambda c: line.put(1, c, times_down(cur[line.rows(c), :], w_ref, 2)))
-    each(N, lambda c: line.exchange(1, c))
-    each(N, lambda c: line.get(1, c))
-    got_w(3)
-
     def v_copy(slot, peer):
         return pltpu.make_async_remote_copy(
             src_ref=v_out.at[peer],
@@ -243,7 +258,23 @@
             v_out[c] = part_v.astype(BF16)
             v_copy(me, c).start()
 
-    each(N, vectors)
+    def middle(c):
+        next_current(0, c)
+        line.put(1, c, times_down(cur[line.rows(c), :], w_ref, 2))
+
+    def second_sum(i):
+        pump(N + 3 + i)
+        stage(i, middle)
+        stage(i, lambda c: line.exchange(1, c))
+        stage(i - line.lag(1, 3), lambda c: line.get(1, c))
+
+        @pl.when(i == 3)
+        def _():
+            got_w(3)
+
+        stage(i - 3, vectors)
+
+    each(N + 3, second_sum)
     vector = v_own[...]
     for d in range(1, N):
         peer = (me + d) % N
@@ -259,11 +290,11 @@
         total = total + dot(pick, vector[:, k * E : (k + 1) * E])
     ordered_ref[...] = total.astype(BF16)
 
-    sent_w(3)
+    send_w(3, 3).wait_send()
     for d in range(1, N):
         v_copy(me, (me + d) % N).wait_send()
     for layer in range(2):
-        each(N, lambda c: line.drain(layer, c))
+        line.drain(layer)
 
 
 def backward_kernel(
@@ -320,9 +351,6 @@
             dscale = (g * x_ref[rows, cols].astype(F32)).astype(BF16)
             total = total + dot(dscale, ranks(w_ref, 3, lo, NB))
         line.put(0, c, total)
-
-    each(N, last_layer)
-    each(N, lambda c: line.exchange(0, c))
 
     def first_layer(c):
         rows = line.rows(c)
@@ -338,9 +366,6 @@
             total = total + dot(dscale, ranks(w_ref, 1, lo, NB))
         line.put(1, c, total)
 
-    each(N, first_layer)
-    each(N, lambda c: line.exchange(1, c))
-
     def finish(c):
         rows = line.rows(c)
         line.get(1, c)
@@ -350,11 +375,70 @@
             g0 = grad[rows, cols] + dot_t(dhidden, ranks(w_ref, 0, lo, NB))
             out_ref[rows, cols] = g0.astype(BF16)
 
-    each(N, finish)
+    def both_sums(i):
+        stage(i, last_layer)
+        stage(i, lambda c: line.exchange(0, c))
+        stage(i - line.lag(1, 3), first_layer)
+        stage(i - 3, lambda c: line.exchange(1, c))
+        stage(i - line.lag(4, 6), finish)
+
+    each(N + 6, both_sums)
     for d in range(1, N):
         v_copy(me, (me + d) % N).wait_send()
     for layer in range(2):
-        each(N, lambda c: line.drain(layer, c))
+        line.drain(layer)
+
+
+def interaction_kernel(vec_ref, cot_ref, table_ref, ret_ref, got, back, sems):
+    towers, packed, _ = vec_ref.shape
+    owned = cot_ref.shape[0]
+    vecs = cot_ref.shape[1]
+    me = lax.axis_index("tower")
+    barrier = pltpu.get_barrier_semaphore()
+
+    def other(d):
+        return (me + 1 + d) % towers
+
+    each(towers - 1, lambda d: pl.semaphore_signal(barrier, inc=1, device_id={"tower": other(d)}))
+    pl.semaphore_wait(barrier, towers - 1)
+
+    def exchange(phase, src, dst):
+        def copy(d):
+            return pltpu.make_async_remote_copy(
+                src_ref=src.at[other(d)],
+                dst_ref=dst.at[me],
+                send_sem=sems.at[0, phase],
+                recv_sem=sems.at[1, phase],
+                device_id={"tower": other(d)},
+            )
+
+        each(towers - 1, lambda d: copy(d).start())
+        dst[me] = src[me]
+
+    def arrived(which, phase, ref):
+        all_but_one = ref.at[pl.ds(0, towers - 1)]
+        pltpu.make_async_copy(all_but_one, all_but_one, sems.at[which, phase]).wait()
+
+    exchange(0, vec_ref, got)
+    arrived(1, 0, got)
+    flat = got[...].reshape(towers * packed, E)
+    shape = (vecs, towers * packed)
+    row = lax.broadcasted_iota(jnp.int32, shape, 0)
+    col = lax.broadcasted_iota(jnp.int32, shape, 1)
+    total = jnp.zeros((towers * packed, E), F32)
+    for r in range(owned):
+        pick = jnp.where(col == (row // 2) * packed + 2 * r + row % 2, 1.0, 0.0).astype(BF16)
+        vectors = dot(pick, flat).astype(BF16)
+        table_ref[r] = dot_t(vectors, vectors) * (1.0 / E)
+        cot = cot_ref[r]
+        both = dot(cot, vectors) + lax.dot_general(cot, vectors, TN, preferred_element_type=F32)
+        grad = (both * (1.0 / E)).astype(BF16)
+        total = total + lax.dot_general(pick, grad, TN, preferred_element_type=F32)
+    back[...] = total.astype(BF16).reshape(towers, packed, E)
+    exchange(1, back, ret_ref)
+    arrived(1, 1, ret_ref)
+    for phase in range(2):
+        arrived(0, phase, got)
 
 
 def line_scratch(samples, rank):
@@ -414,15 +498,16 @@
         cross_bias[0].reshape(2, slots, 1, E), projector[0].reshape(slots, E, 2 * E),
     )
 
-    owned = lax.all_to_all(ordered.reshape(towers, 8, E), "tower", split_axis=0, concat_axis=0, tiled=True)
-    vectors = owned.reshape(towers, 4, 2, E).transpose(1, 0, 2, 3).reshape(4, 2 * towers, E)
-    table = jnp.einsum("bie,bje->bij", vectors, vectors, preferred_element_type=F32) / E
+    table, returned = pl.pallas_call(
+        interaction_kernel,
+        out_shape=(sds((4, 2 * towers, 2 * towers), F32), sds((towers, 8, E), BF16)),
+        in_specs=[vmem()] * 2,
+        out_specs=(vmem(),) * 2,
+        scratch_shapes=[pltpu.VMEM((towers, 8, E), BF16)] * 2 + [pltpu.SemaphoreType.DMA((2, 2))],
+        compiler_params=params(2),
+        name="interaction",
+    )(ordered.reshape(towers, 8, E), inter_grad.reshape(4, 2 * towers, 2 * towers))
     interactions = table.reshape(4, -1)
-    cot = inter_grad.astype(F32).reshape(4, 2 * towers, 2 * towers)
-    symmetric = cot + jnp.swapaxes(cot, 1, 2)
-    vec_grad = (jnp.einsum("bij,bje->bie", symmetric, vectors.astype(F32)) / E).astype(BF16)
-    back = vec_grad.reshape(4, towers, 2, E).transpose(1, 0, 2, 3).reshape(towers, 8, E)
-    returned = lax.all_to_all(back, "tower", split_axis=0, concat_axis=0, tiled=True)
 
     slab_grad = pl.pallas_call(
         backward_kernel,

time: 346 us -> 307 us (0.89)
  waiting for transfers between devices: 21.1 us -> 0 us
  starting transfers between devices: 16.1 us -> 0 us
    pallas_call x0 -> x1, Pallas kernels: none -> 27.7 us  [per_device(): pl.pallas_call(interaction_kernel, out_shape=(sds((4, 2 * towers, 2 * tow...]
    all_to_all x2 -> x0, waiting for transfers between devices: 21.1 us -> none  [the longest x1 11.3 us: per_device(): lax.all_to_all(ordered.reshape(towers, 8, E), 'tower', split_axis=0, conc...]
    all_to_all x2 -> x0, starting transfers between devices: 16.1 us -> none  [the longest x1 10.4 us: per_device(): lax.all_to_all(ordered.reshape(towers, 8, E), 'tower', split_axis=0, conc...]
    pallas_call x1, Pallas kernels: 101 us -> 85.6 us  [per_device(): pl.pallas_call(backward_kernel, out_shape=sds((samples, width), BF16), in...]
    pallas_call x1, Pallas kernels: 196 us -> 182 us  [per_device(): pl.pallas_call(forward_kernel, out_shape=(sds((2 * block, E), BF16), sds(...]
  transfers between devices with their start and end apart: 2 -> 0, of which waited for: 2 -> 0; matrix products, arithmetic and copies ran while one was open for 1% -> 0% of each run, Pallas kernels for 0% -> 0%
where the time goes in v2:
time: 307 us; the launch traced here: 306 us
  Pallas kernels  295 us (96%)
  local copies, waits for them, and re-layouts  9.55 us (3%)
    pallas_call x1, Pallas kernels, per_device(): pl.pallas_call(forward_kernel, out_shape=(sds((2 * block, E), BF16), sds(...  182 us
    pallas_call x1, Pallas kernels, per_device(): pl.pallas_call(backward_kernel, out_shape=sds((samples, width), BF16), in...  85.6 us
    pallas_call x1, Pallas kernels, per_device(): pl.pallas_call(interaction_kernel, out_shape=(sds((4, 2 * towers, 2 * tow...  27.7 us
    unnamed x5, local copies, waits for them, and re-layouts  6.49 us

profile of v2, /device:TPU:2, one launch (start us, length us, event | category | flops | bytes accessed | tf_op | source)
XLA Modules:
  0.0 306.5 jit_solution(14710023618549491644)
XLA Ops:
  0.6 0.0 copy-start
  0.6 1.3 select_reduce_fusion.inv_ref
  2.0 0.0 copy-done
  2.0 1.4 reshape_squeeze.14.bias_ref
  3.4 0.1 broadcast_in_dim.22
  3.5 0.7 broadcast_in_dim_reshape.7.own_ref
  4.2 0.8 broadcast_in_dim_reshape.8.own_ref
  5.1 1.6 copy.17
  6.6 181.6 %forward.1 = (bf16[512,128]{1,0:T(8,128)(2,1)}, bf16[4,4,1024,128]{3,2,1,0:T(8,128)(2,1)}, bf16[1024,256]{1,0:T(8,128)(2,1)}, bf16[2,1024,512]{2,1,0:T(8,128)(2,1)}, f32[2,1,1024]{2,1,0:T(1,128)}) custom-call(s32[32]{0:T(128)} %select_reduce_fusion.inv_ref, s32[512,1]{1,0:T(8,128)} %broadcast_in_dim_reshape.8.own_ref, bf16[1024,1024]{1,0:T(8,128)(2,1)} %bitcast.17, ...), custom_call_target="tpu_custom_call" | custom-call | tf_op jit(solution)/shard_map/forward/pallas_call | solution.py:471
  188.2 27.7 %interaction.1 = (f32[4,128,128]{2,1,0:T(8,128)}, bf16[64,8,128]{2,1,0:T(8,128)(2,1)}) custom-call(bf16[64,8,128]{2,1,0:T(8,128)(2,1)} %bitcast.28, bf16[4,128,128]{2,1,0:T(8,128)(2,1)} %bitcast.23), custom_call_target="tpu_custom_call" | custom-call | tf_op jit(solution)/shard_map/interaction/pallas_call | solution.py:501
  216.0 1.8 copy.16
  217.8 85.6 %backward.1 = bf16[1024,1024]{1,0:T(8,128)(2,1)} custom-call(s32[1,512]{1,0:T(1,128)} %broadcast_in_dim_reshape.7.own_ref, bf16[512,128]{1,0:T(8,128)(2,1)} %bitcast.26, bf16[1024,1024]{1,0:T(8,128)(2,1)} %bitcast.18, bf16[4,4,1024,128]{3,2,1,0:T(8,128)(2,1)} %get-tuple-element.12.w_ref, bf16[1024,256]{1,0:T(8,128)(2,1)} %get-tuple-element.13.pw_ref, ...), custom_call_target="tpu_custom_call" | custom-call | tf_op jit(solution)/shard_map/backward/pallas_call | solution.py:512
  303.4 3.1 %copy.19 = bf16[1,1024,1024]{2,1,0:T(8,128)(2,1)} copy(bf16[1,1024,1024]{2,1,0:T(8,128)(2,1)} %bitcast.19) | data formatting | bytes 4194304
  (1 shorter events, 0.0 us)
Async XLA Ops:
  0.6 1.4 copy-start

commit v3 on v1

v3 whole, which is shorter than its diff:
```python
import jax
import jax.numpy as jnp
from jax import lax
from jax.experimental import pallas as pl
from jax.experimental.pallas import tpu as pltpu
from jax.sharding import PartitionSpec as P

F32 = jnp.float32
BF16 = jnp.bfloat16
E = 128
N = 4
PUMPS = ((1, 0), (2, 2), (3, 5))
NB = 256
NT = (((1,), (1,)), ((), ()))
TN = (((0,), (0,)), ((), ()))


def dot(a, b):
    return jnp.dot(a, b, preferred_element_type=F32)


def dot_t(a, b):
    return lax.dot_general(a, b, NT, preferred_element_type=F32)


def line_position():
    me = lax.axis_index("member")
    near = me + 1 - 2 * (me % 2)
    hub = ((me + 1) // 2) % 2
    return me, near, 3 - me, hub


class LineSum:
    def __init__(self, block, total, own, mine, from_end, from_side, sems):
        self.me, self.near, self.across, self.hub = line_position()
        self.block, self.total, self.own = block, total, own
        self.mine, self.from_end, self.from_side = mine, from_end, from_side
        self.sems = sems

    def rows(self, c):
        return pl.ds(pl.multiple_of(c * self.block, self.block), self.block)

    def copy(self, kind, src, dst, n, c, peer):
        rows = self.rows(c)
        return pltpu.make_async_remote_copy(
            src_ref=src.at[n, rows],
            dst_ref=dst.at[n, rows],
            send_sem=self.sems.at[2 * kind, n, c],
            recv_sem=self.sems.at[2 * kind + 1, n, c],
            device_id={"member": peer},
        )

    def to_hub(self, n, c):
        return self.copy(0, self.mine, self.from_end, n, c, self.near)

    def to_side(self, n, c):
        return self.copy(1, self.mine, self.from_side, n, c, self.across)

    def to_end(self, n, c):
        return self.copy(2, self.total, self.total, n, c, self.near)

    def put(self, n, c, value):
        @pl.when(self.hub == 1)
        def _():
            self.own[self.rows(c), :] = value

        @pl.when(self.hub == 0)
        def _():
            self.mine[n, self.rows(c), :] = value.astype(BF16)

            @pl.when(c > 0)
            def _():
                self.to_hub(n, c - 1).wait_send()

            self.to_hub(n, c).start()

    def exchange(self, n, c):
        rows = self.rows(c)

        @pl.when(self.hub == 1)
        def _():
            self.to_hub(n, c).wait_recv()
            both = self.own[rows, :] + self.from_end[n, rows, :].astype(F32)
            self.mine[n, rows, :] = both.astype(BF16)
            self.to_side(n, c).start()

    def get(self, n, c):
        rows = self.rows(c)

        @pl.when(self.hub == 1)
        def _():
            self.to_side(n, c).wait_recv()
            whole = self.mine[n, rows, :].astype(F32) + self.from_side[n, rows, :].astype(F32)
            self.total[n, rows, :] = whole.astype(BF16)
            self.to_end(n, c).start()

        @pl.when(self.hub == 0)
        def _():
            self.to_end(n, c).wait_recv()

    def lag(self, hub, end):
        return hub * self.hub + end * (1 - self.hub)

    def drain(self, n):
        @pl.when(self.hub == 1)
        def _():
            def both(c):
                self.to_side(n, c).wait_send()
                self.to_end(n, c).wait_send()

            each(N, both)

        @pl.when(self.hub == 0)
        def _():
            self.to_hub(n, N - 1).wait_send()


def each(count, body):
    lax.fori_loop(0, count, lambda i, _: (body(i), 0)[1], 0)


def stage(c, body):
    @pl.when((c >= 0) & (c < N))
    def _():
        body(c)


def ranks(w_ref, k, lo, rows):
    return jnp.concatenate([w_ref[k, r, lo : lo + rows, :] for r in range(N)], axis=1)


def times_down(a, w_ref, k):
    width = w_ref.shape[2]
    halves = []
    for j in range(0, N, 2):
        right = jnp.concatenate([w_ref[k, j], w_ref[k, j + 1]], axis=1)
        halves.append(dot(a, right))
    return jnp.concatenate(halves, axis=1)


def step_kernel(
    inv_ref, own_col_ref, own_row_ref, x_hbm, down_hbm, up_hbm, bias_ref, proj_hbm, cot_ref,
    out_ref, table_ref,
    x_ref, map0, map1, map2, map3, proj_ref, ready, w_ref, pw_ref, bw_ref, cur, scales, grad,
    own, total_ref, mine, from_end, from_side, v_out, v_own, v_in, vg, ordered, got, back, ret,
    load_sems, sems, w_sems, v_sems, g_sems, t_sems,
):
    samples, width = x_ref.shape
    block = samples // N
    rank = N * E
    feats = width // E
    towers, packed, _ = ordered.shape
    owned, vecs = cot_ref.shape[:2]
    line = LineSum(block, total_ref, own, mine, from_end, from_side, sems)
    me = line.me
    tower = lax.axis_index("tower")

    def other(d):
        return (tower + 1 + d) % towers

    loads = [
        pltpu.make_async_copy(src, dst, load_sems.at[i])
        for i, (src, dst) in enumerate(
            (
                (down_hbm.at[0], map0),
                (x_hbm, x_ref),
                (up_hbm.at[0], map1),
                (down_hbm.at[1], map2),
                (up_hbm.at[1], map3),
                (proj_hbm, proj_ref),
            )
        )
    ]
    for load in loads:
        load.start()
    barrier = pltpu.get_barrier_semaphore()
    for d in range(1, N):
        pl.semaphore_signal(barrier, inc=1, device_id={"member": (me + d) % N})
    each(towers - 1, lambda d: pl.semaphore_signal(barrier, inc=1, device_id={"tower": other(d)}))

    def send_w(k, d):
        peer = (me + d) % N
        return pltpu.make_async_remote_copy(
            src_ref=ready.at[k, peer],
            dst_ref=w_ref.at[k, me],
            send_sem=w_sems.at[0, k, peer],
            recv_sem=w_sems.at[1, k, me],
            device_id={"member": peer},
        )

    def recv_w(k, d):
        peer = (me + d) % N
        return pltpu.make_async_remote_copy(
            src_ref=ready.at[k, peer],
            dst_ref=w_ref.at[k, peer],
            send_sem=w_sems.at[0, k, peer],
            recv_sem=w_sems.at[1, k, peer],
            device_id={"member": peer},
        )

    def make_ready(k):
        source = (map0, map1, map2, map3)[k]

        def one(f):
            at = pl.multiple_of((f % feats) * E, E)
            ready[k, f // feats, pl.ds(at, E), :] = source[inv_ref[f]]

        each(N * feats, one)
        w_ref[k, me] = ready[k, me]

    def start_w(k):
        for d in range(1, N):
            send_w(k, d).start()

    def sent_w(k):
        for d in range(1, N):
            send_w(k, d).wait_send()

    def got_w(k):
        for d in range(1, N):
            recv_w(k, d).wait_recv()

    def pump(i):
        for k, at in PUMPS:

            @pl.when(i == at)
            def _():
                if k > 1:
                    sent_w(k - 1)
                start_w(k)

    loads[0].wait()
    make_ready(0)
    pl.semaphore_wait(barrier, N - 1 + towers - 1)
    start_w(0)
    for load in loads[1:]:
        load.wait()
    for k in range(1, 4):
        make_ready(k)
    for i in range(feats):
        slot = inv_ref[me * feats + i]
        pw_ref[i * E : (i + 1) * E, :] = proj_ref[slot]
        for layer in range(2):
            bw_ref[layer, :, i * E : (i + 1) * E] = bias_ref[layer, slot]
    sent_w(0)
    got_w(0)

    def first_sum(i):
        pump(i)
        stage(i, lambda c: line.put(0, c, times_down(x_ref[line.rows(c), :], w_ref, 0)))
        stage(i, lambda c: line.exchange(0, c))
        stage(i - line.lag(1, 3), lambda c: line.get(0, c))

    each(N + 3, first_sum)
    got_w(1)
    got_w(2)

    def next_current(layer, c):
        rows = line.rows(c)
        hidden = total_ref[layer, rows, :]
        for lo in range(0, width, NB):
            cols = slice(lo, lo + NB)
            scale = dot_t(hidden, ranks(w_ref, 2 * layer + 1, lo, NB)) + bw_ref[layer, :, cols]
            scales[layer, rows, cols] = scale
            x = x_ref[rows, cols].astype(F32)
            before = x if layer == 0 else cur[rows, cols].astype(F32)
            cur[rows, cols] = (x * scale + before).astype(BF16)

    def v_copy(slot, peer):
        return pltpu.make_async_remote_copy(
            src_ref=v_out.at[peer],
            dst_ref=v_in.at[slot],
            send_sem=v_sems.at[0, peer],
            recv_sem=v_sems.at[1, slot],
            device_id={"member": peer},
        )

    def vectors(c):
        next_current(1, c)
        part_v = dot(cur[line.rows(c), :], pw_ref[...])

        @pl.when(c == me)
        def _():
            v_own[...] = part_v

        @pl.when(c != me)
        def _():
            v_out[c] = part_v.astype(BF16)
            v_copy(me, c).start()

    def middle(c):
        next_current(0, c)
        line.put(1, c, times_down(cur[line.rows(c), :], w_ref, 2))

    def second_sum(i):
        pump(N + 3 + i)
        stage(i, middle)
        stage(i, lambda c: line.exchange(1, c))
        stage(i - line.lag(1, 3), lambda c: line.get(1, c))

        @pl.when(i == 3)
        def _():
            got_w(3)

        stage(i - 3, vectors)

    each(N + 3, second_sum)
    vector = v_own[...]
    for d in range(1, N):
        peer = (me + d) % N
        v_copy(peer, peer).wait_recv()
        vector = vector + v_in[peer].astype(F32)
    vector = vector.astype(BF16)
    shape = (2 * block, block)
    hit = own_col_ref[...] == lax.broadcasted_iota(jnp.int32, shape, 1)
    odd = lax.broadcasted_iota(jnp.int32, shape, 0) % 2
    total = jnp.zeros((2 * block, E), F32)
    for k in range(2):
        pick = jnp.where(hit & (odd == k), 1.0, 0.0).astype(BF16)
        total = total + dot(pick, vector[:, k * E : (k + 1) * E])
    ordered[...] = total.astype(BF16).reshape(towers, packed, E)

    def swap(phase, src, dst):
        def copy(d):
            return pltpu.make_async_remote_copy(
                src_ref=src.at[other(d)],
                dst_ref=dst.at[tower],
                send_sem=t_sems.at[0, phase],
                recv_sem=t_sems.at[1, phase],
                device_id={"tower": other(d)},
            )

        each(towers - 1, lambda d: copy(d).start())
        dst[tower] = src[tower]

    def arrived(which, phase, ref):
        all_but_one = ref.at[pl.ds(0, towers - 1)]
        pltpu.make_async_copy(all_but_one, all_but_one, t_sems.at[which, phase]).wait()

    swap(0, ordered, got)
    shape = (vecs, towers * packed)
    row = lax.broadcasted_iota(jnp.int32, shape, 0)
    col = lax.broadcasted_iota(jnp.int32, shape, 1)
    arrived(1, 0, got)
    flat = got[...].reshape(towers * packed, E)
    total = jnp.zeros((towers * packed, E), F32)
    held = []
    for r in range(owned):
        pick = jnp.where(col == (row // 2) * packed + 2 * r + row % 2, 1.0, 0.0).astype(BF16)
        vecs_r = dot(pick, flat).astype(BF16)
        held.append(vecs_r)
        cot = cot_ref[r]
        both = dot(cot, vecs_r) + lax.dot_general(cot, vecs_r, TN, preferred_element_type=F32)
        g = (both * (1.0 / E)).astype(BF16)
        total = total + lax.dot_general(pick, g, TN, preferred_element_type=F32)
    back[...] = total.astype(BF16).reshape(towers, packed, E)
    swap(1, back, ret)
    for r in range(owned):
        table_ref[r] = dot_t(held[r], held[r]) * (1.0 / E)
    arrived(1, 1, ret)

    shape = (block, 2 * block)
    hit = own_row_ref[...] == lax.broadcasted_iota(jnp.int32, shape, 0)
    odd = lax.broadcasted_iota(jnp.int32, shape, 1) % 2
    flat = ret[...].reshape(towers * packed, E)
    for k in range(2):
        pick = jnp.where(hit & (odd == k), 1.0, 0.0).astype(BF16)
        vg[me, :, k * E : (k + 1) * E] = dot(pick, flat).astype(BF16)

    def g_copy(slot, peer):
        return pltpu.make_async_remote_copy(
            src_ref=vg.at[slot],
            dst_ref=vg.at[slot],
            send_sem=g_sems.at[0, peer],
            recv_sem=g_sems.at[1, slot],
            device_id={"member": peer},
        )

    for d in range(1, N):
        g_copy(me, (me + d) % N).start()

    def last_layer(c):
        rows = line.rows(c)

        @pl.when(c != me)
        def _():
            g_copy(c, c).wait_recv()

        total = jnp.zeros((block, rank), F32)
        for lo in range(0, width, NB):
            cols = slice(lo, lo + NB)
            g = dot_t(vg[c], pw_ref[cols, :])
            grad[rows, cols] = g
            dscale = (g * x_ref[rows, cols].astype(F32)).astype(BF16)
            total = total + dot(dscale, ranks(w_ref, 3, lo, NB))
        line.put(2, c, total)

    def first_layer(c):
        rows = line.rows(c)
        line.get(2, c)
        dhidden = total_ref[2, rows, :]
        total = jnp.zeros((block, rank), F32)
        for lo in range(0, width, NB):
            cols = slice(lo, lo + NB)
            g2 = grad[rows, cols]
            g1 = g2 + dot_t(dhidden, ranks(w_ref, 2, lo, NB))
            grad[rows, cols] = g1 + (g2 * scales[1, rows, cols] + g1 * scales[0, rows, cols])
            dscale = (g1 * x_ref[rows, cols].astype(F32)).astype(BF16)
            total = total + dot(dscale, ranks(w_ref, 1, lo, NB))
        line.put(3, c, total)

    def finish(c):
        rows = line.rows(c)
        line.get(3, c)
        dhidden = total_ref[3, rows, :]
        for lo in range(0, width, NB):
            cols = slice(lo, lo + NB)
            g0 = grad[rows, cols] + dot_t(dhidden, ranks(w_ref, 0, lo, NB))
            out_ref[rows, cols] = g0.astype(BF16)

    def both_sums(i):
        stage(i, last_layer)
        stage(i, lambda c: line.exchange(2, c))
        stage(i - line.lag(1, 3), first_layer)
        stage(i - 3, lambda c: line.exchange(3, c))
        stage(i - line.lag(4, 6), finish)

    each(N + 6, both_sums)

    sent_w(3)
    for d in range(1, N):
        v_copy(me, (me + d) % N).wait_send()
        g_copy(me, (me + d) % N).wait_send()
    for phase in range(2):
        arrived(0, phase, got)
    for n in range(4):
        line.drain(n)


def vmem():
    return pl.BlockSpec(memory_space=pltpu.VMEM)


def params(collective_id):
    return pltpu.CompilerParams(
        collective_id=collective_id, has_side_effects=True, vmem_limit_bytes=62 << 20
    )


def per_device(slabs, cross_down, cross_up, cross_bias, projector, placement, owner, inter_grad):
    x = slabs[0]
    samples, width = x.shape
    block = samples // N
    slots = placement.shape[1]
    rank = N * cross_down.shape[3]
    towers = block // 4
    order = placement[0]
    index = jnp.arange(slots, dtype=jnp.int32)
    inverse = jnp.sum(jnp.where(order[None, :] == index[:, None], index[None, :], 0), axis=1)
    own_row = lax.dynamic_index_in_dim(owner, lax.axis_index("member"), 0, keepdims=False)
    own_twice = jnp.repeat(own_row, 2)
    sds = jax.ShapeDtypeStruct
    dma = pltpu.SemaphoreType.DMA
    any_spec = pl.BlockSpec(memory_space=pl.ANY)
    slab_grad, table = pl.pallas_call(
        step_kernel,
        out_shape=(sds((samples, width), BF16), sds((4, 2 * towers, 2 * towers), F32)),
        in_specs=[
            pl.BlockSpec(memory_space=pltpu.SMEM), vmem(), vmem(), any_spec, any_spec, any_spec,
            vmem(), any_spec, vmem(),
        ],
        out_specs=(vmem(),) * 2,
        scratch_shapes=[
            pltpu.VMEM((samples, width), BF16),
            *[pltpu.VMEM((slots, E, E), BF16)] * 4,
            pltpu.VMEM((slots, E, 2 * E), BF16),
            pltpu.VMEM((4, N, width, E), BF16),
            pltpu.VMEM((4, N, width, E), BF16),
            pltpu.VMEM((width, 2 * E), BF16),
            pltpu.VMEM((2, 1, width), F32),
            pltpu.VMEM((samples, width), BF16),
            pltpu.VMEM((2, samples, width), F32),
            pltpu.VMEM((samples, width), F32),
            pltpu.VMEM((samples, rank), F32),
            *[pltpu.VMEM((4, samples, rank), BF16)] * 4,
            pltpu.VMEM((N, block, 2 * E), BF16),
            pltpu.VMEM((block, 2 * E), F32),
            pltpu.VMEM((N, block, 2 * E), BF16),
            pltpu.VMEM((N, block, 2 * E), BF16),
            *[pltpu.VMEM((towers, 8, E), BF16)] * 4,
            dma((6,)),
            dma((6, 4, N)),
            dma((2, 4, N)),
            dma((2, N)),
            dma((2, N)),
            dma((2, 2)),
        ],
        compiler_params=params(0),
        name="mega",
    )(
        inverse, own_twice[:, None], own_twice[None, :], x,
        cross_down[0].reshape(2, slots, E, E), cross_up[0].reshape(2, slots, E, E),
        cross_bias[0].reshape(2, slots, 1, E), projector[0].reshape(slots, E, 2 * E),
        inter_grad.reshape(4, 2 * towers, 2 * towers),
    )
    interactions = table.reshape(4, -1)
    return interactions, slab_grad[None]


def solution(mesh):
    placed = (
        P("tower", None, "member"),
        P("tower", None, None, "member"),
        P("tower", None, None, "member"),
        P("tower", None, None),
        P("tower", None, None),
        P("tower", None),
        P(),
        P(("tower", "member"), None),
    )
    return jax.shard_map(
        per_device,
        mesh=mesh,
        in_specs=placed,
        out_specs=(P(("tower", "member"), None), P("tower", None, "member")),
        check_vma=False,
    )
```

time: 346 us -> 287 us (0.83)
  Pallas kernels: 297 us -> 275 us
  waiting for transfers between devices: 21.1 us -> 0 us
  starting transfers between devices: 16.1 us -> 0 us
    pallas_call x2 -> x1, Pallas kernels: 297 us -> 275 us  [per_device(): pl.pallas_call(step_kernel, out_shape=(sds((samples, width), BF16), sds((...]
    all_to_all x2 -> x0, waiting for transfers between devices: 21.1 us -> none  [the longest x1 11.3 us: per_device(): lax.all_to_all(ordered.reshape(towers, 8, E), 'tower', split_axis=0, conc...]
    all_to_all x2 -> x0, starting transfers between devices: 16.1 us -> none  [the longest x1 10.4 us: per_device(): lax.all_to_all(ordered.reshape(towers, 8, E), 'tower', split_axis=0, conc...]
  transfers between devices with their start and end apart: 2 -> 0, of which waited for: 2 -> 0; matrix products, arithmetic and copies ran while one was open for 1% -> 0% of each run, Pallas kernels for 0% -> 0%
where the time goes in v3:
time: 287 us; the launch traced here: 286 us
  Pallas kernels  275 us (96%)
  local copies, waits for them, and re-layouts  9.54 us (3%)
    pallas_call x1, Pallas kernels, per_device(): pl.pallas_call(step_kernel, out_shape=(sds((samples, width), BF16), sds((...  275 us
    unnamed x5, local copies, waits for them, and re-layouts  6.49 us

profile of v3, /device:TPU:2, one launch (start us, length us, event | category | flops | bytes accessed | tf_op | source)
XLA Modules:
  0.0 286.4 jit_solution(9856072716817742597)
XLA Ops:
  0.6 0.0 copy-start
  0.6 1.3 select_reduce_fusion.inv_ref
  1.9 0.0 copy-done
  1.9 1.4 reshape_squeeze.14.bias_ref
  3.3 0.1 broadcast_in_dim.22
  3.4 0.7 broadcast_in_dim_reshape.7.own_row_ref
  4.2 0.8 broadcast_in_dim_reshape.8.own_col_ref
  5.0 1.6 copy.17
  6.6 274.9 %mega.1 = (bf16[1024,1024]{1,0:T(8,128)(2,1)}, f32[4,128,128]{2,1,0:T(8,128)}) custom-call(s32[32]{0:T(128)} %select_reduce_fusion.inv_ref, s32[512,1]{1,0:T(8,128)} %broadcast_in_dim_reshape.8.own_col_ref, s32[1,512]{1,0:T(1,128)} %broadcast_in_dim_reshape.7.own_row_ref, bf16[1024,1024]{1,0:T(8,128)(2,1)} %bitcast.15, bf16[2,32,128,128]{3,2,1,0:T(8,128)(2,1)} %bitcast.16, ...), custom_call_target="tpu_custom_call" | custom-call | tf_op jit(solution)/shard_map/mega/pallas_call | solution.py:465
  281.5 1.8 copy.16
  283.3 3.1 %copy.19 = bf16[1,1024,1024]{2,1,0:T(8,128)(2,1)} copy(bf16[1,1024,1024]{2,1,0:T(8,128)(2,1)} %bitcast.19) | data formatting | bytes 4194304
  (1 shorter events, 0.0 us)
Async XLA Ops:
  0.6 1.3 copy-start

commit v4 on v3

--- a/solution.py
+++ b/solution.py
@@ -9,7 +9,7 @@
 BF16 = jnp.bfloat16
 E = 128
 N = 4
-PUMPS = ((1, 0), (2, 2), (3, 5))
+PUMPS = ((1, 0), (2, 4), (3, 7))
 NB = 256
 NT = (((1,), (1,)), ((), ()))
 TN = (((0,), (0,)), ((), ()))
@@ -139,10 +139,11 @@
 
 
 def step_kernel(
-    inv_ref, own_col_ref, own_row_ref, x_hbm, down_hbm, up_hbm, bias_ref, proj_hbm, cot_ref,
-    out_ref, table_ref,
+    inv_ref, owner_ref, x_hbm, down_hbm, up_hbm, bias_ref, proj_hbm, cot_ref,
+    out_ref, inter_ref,
     x_ref, map0, map1, map2, map3, proj_ref, ready, w_ref, pw_ref, bw_ref, cur, scales, grad,
     own, total_ref, mine, from_end, from_side, v_out, v_own, v_in, vg, ordered, got, back, ret,
+    bias_slots, picks, cots, tables,
     load_sems, sems, w_sems, v_sems, g_sems, t_sems,
 ):
     samples, width = x_ref.shape
@@ -150,7 +151,7 @@
     rank = N * E
     feats = width // E
     towers, packed, _ = ordered.shape
-    owned, vecs = cot_ref.shape[:2]
+    vecs, owned, _ = cots.shape
     line = LineSum(block, total_ref, own, mine, from_end, from_side, sems)
     me = line.me
     tower = lax.axis_index("tower")
@@ -237,11 +238,24 @@
         load.wait()
     for k in range(1, 4):
         make_ready(k)
+    for j in range(N * feats):
+        bias_slots[j] = bias_ref[:, j * E : (j + 1) * E]
     for i in range(feats):
         slot = inv_ref[me * feats + i]
         pw_ref[i * E : (i + 1) * E, :] = proj_ref[slot]
+        bias = bias_slots[slot]
         for layer in range(2):
-            bw_ref[layer, :, i * E : (i + 1) * E] = bias_ref[layer, slot]
+            bw_ref[layer, :, i * E : (i + 1) * E] = bias[layer : layer + 1]
+    places = lax.broadcasted_iota(jnp.int32, (block, block), 0)
+    owns = jnp.where(owner_ref[pl.ds(me, 1), :] == places, 1.0, 0.0).astype(BF16)
+    shape = (2 * block, block)
+    row = lax.broadcasted_iota(jnp.int32, shape, 0)
+    col = lax.broadcasted_iota(jnp.int32, shape, 1)
+    for k in range(2):
+        spread = jnp.where(row == 2 * col + k, 1.0, 0.0).astype(BF16)
+        picks[k] = dot_t(spread, owns).astype(BF16)
+    for i in range(vecs):
+        cots[i] = cot_ref[:, i * E : (i + 1) * E].astype(F32)
     sent_w(0)
     got_w(0)
 
@@ -311,13 +325,9 @@
         v_copy(peer, peer).wait_recv()
         vector = vector + v_in[peer].astype(F32)
     vector = vector.astype(BF16)
-    shape = (2 * block, block)
-    hit = own_col_ref[...] == lax.broadcasted_iota(jnp.int32, shape, 1)
-    odd = lax.broadcasted_iota(jnp.int32, shape, 0) % 2
     total = jnp.zeros((2 * block, E), F32)
     for k in range(2):
-        pick = jnp.where(hit & (odd == k), 1.0, 0.0).astype(BF16)
-        total = total + dot(pick, vector[:, k * E : (k + 1) * E])
+        total = total + dot(picks[k], vector[:, k * E : (k + 1) * E])
     ordered[...] = total.astype(BF16).reshape(towers, packed, E)
 
     def swap(phase, src, dst):
@@ -349,23 +359,23 @@
         pick = jnp.where(col == (row // 2) * packed + 2 * r + row % 2, 1.0, 0.0).astype(BF16)
         vecs_r = dot(pick, flat).astype(BF16)
         held.append(vecs_r)
-        cot = cot_ref[r]
+        cot = cots[:, r, :].astype(BF16)
         both = dot(cot, vecs_r) + lax.dot_general(cot, vecs_r, TN, preferred_element_type=F32)
         g = (both * (1.0 / E)).astype(BF16)
         total = total + lax.dot_general(pick, g, TN, preferred_element_type=F32)
     back[...] = total.astype(BF16).reshape(towers, packed, E)
     swap(1, back, ret)
     for r in range(owned):
-        table_ref[r] = dot_t(held[r], held[r]) * (1.0 / E)
+        tables[:, r, :] = dot_t(held[r], held[r]) * (1.0 / E)
+    for i in range(vecs):
+        inter_ref[:, i * E : (i + 1) * E] = tables[i]
     arrived(1, 1, ret)
 
-    shape = (block, 2 * block)
-    hit = own_row_ref[...] == lax.broadcasted_iota(jnp.int32, shape, 0)
-    odd = lax.broadcasted_iota(jnp.int32, shape, 1) % 2
     flat = ret[...].reshape(towers * packed, E)
     for k in range(2):
-        pick = jnp.where(hit & (odd == k), 1.0, 0.0).astype(BF16)
-        vg[me, :, k * E : (k + 1) * E] = dot(pick, flat).astype(BF16)
+        vg[me, :, k * E : (k + 1) * E] = lax.dot_general(
+            picks[k], flat, TN, preferred_element_type=F32
+        ).astype(BF16)
 
     def g_copy(slot, peer):
         return pltpu.make_async_remote_copy(
@@ -457,16 +467,14 @@
     order = placement[0]
     index = jnp.arange(slots, dtype=jnp.int32)
     inverse = jnp.sum(jnp.where(order[None, :] == index[:, None], index[None, :], 0), axis=1)
-    own_row = lax.dynamic_index_in_dim(owner, lax.axis_index("member"), 0, keepdims=False)
-    own_twice = jnp.repeat(own_row, 2)
     sds = jax.ShapeDtypeStruct
     dma = pltpu.SemaphoreType.DMA
     any_spec = pl.BlockSpec(memory_space=pl.ANY)
-    slab_grad, table = pl.pallas_call(
+    slab_grad, interactions = pl.pallas_call(
         step_kernel,
-        out_shape=(sds((samples, width), BF16), sds((4, 2 * towers, 2 * towers), F32)),
+        out_shape=(sds((samples, width), BF16), sds(inter_grad.shape, F32)),
         in_specs=[
-            pl.BlockSpec(memory_space=pltpu.SMEM), vmem(), vmem(), any_spec, any_spec, any_spec,
+            pl.BlockSpec(memory_space=pltpu.SMEM), vmem(), any_spec, any_spec, any_spec,
             vmem(), any_spec, vmem(),
         ],
         out_specs=(vmem(),) * 2,
@@ -488,6 +496,9 @@
             pltpu.VMEM((N, block, 2 * E), BF16),
             pltpu.VMEM((N, block, 2 * E), BF16),
             *[pltpu.VMEM((towers, 8, E), BF16)] * 4,
+            pltpu.VMEM((slots, 2, E), F32),
+            pltpu.VMEM((2, 2 * block, block), BF16),
+            *[pltpu.VMEM((2 * towers, inter_grad.shape[0], E), F32)] * 2,
             dma((6,)),
             dma((6, 4, N)),
             dma((2, 4, N)),
@@ -498,12 +509,10 @@
         compiler_params=params(0),
         name="mega",
     )(
-        inverse, own_twice[:, None], own_twice[None, :], x,
+        inverse, owner, x,
         cross_down[0].reshape(2, slots, E, E), cross_up[0].reshape(2, slots, E, E),
-        cross_bias[0].reshape(2, slots, 1, E), projector[0].reshape(slots, E, 2 * E),
-        inter_grad.reshape(4, 2 * towers, 2 * towers),
+        cross_bias[0], projector[0].reshape(slots, E, 2 * E), inter_grad,
     )
-    interactions = table.reshape(4, -1)
     return interactions, slab_grad[None]
 
 

time: 287 us -> 278 us (0.969)
  local copies, waits for them, and re-layouts: 9.54 us -> 4.75 us
  Pallas kernels: 275 us -> 271 us
    pallas_call x1, Pallas kernels: 275 us -> 271 us  [per_device(): pl.pallas_call(step_kernel, out_shape=(sds((samples, width), BF16), sds(i...]
    another operation x3 -> x0, local copies, waits for them, and re-layouts: 2.96 us -> none  [the longest x1 1.41 us: per_device(): cross_bias[0].reshape(2, slots, 1, E)]
    unnamed x5 -> x2, local copies, waits for them, and re-layouts: 6.49 us -> 4.75 us
where the time goes in v4:
time: 278 us
  Pallas kernels  271 us (97%)
  local copies, waits for them, and re-layouts  4.75 us (2%)
    pallas_call x1, Pallas kernels, per_device(): pl.pallas_call(step_kernel, out_shape=(sds((samples, width), BF16), sds(i...  271 us

profile of v4, /device:TPU:2, one launch (start us, length us, event | category | flops | bytes accessed | tf_op | source)
XLA Modules:
  0.0 278.1 jit_solution(7611882573534981869)
XLA Ops:
  0.6 1.3 select_reduce_fusion.inv_ref
  1.9 271.5 %mega.1 = (bf16[1024,1024]{1,0:T(8,128)(2,1)}, f32[4,16384]{1,0:T(4,128)}) custom-call(s32[32]{0:T(128)} %select_reduce_fusion.inv_ref, s32[4,256]{1,0:T(4,128)} %owner_ref.1, bf16[1024,1024]{1,0:T(8,128)(2,1)} %bitcast.8, bf16[2,32,128,128]{3,2,1,0:T(8,128)(2,1)} %bitcast.9, bf16[2,32,128,128]{3,2,1,0:T(8,128)(2,1)} %bitcast.10, f32[2,4096]{1,0:T(2,128)} %bitcast.12, ...), custom_call_target="tpu_custom_call" | custom-call | tf_op jit(solution)/shard_map/mega/pallas_call | solution.py:473
  273.4 1.7 copy.12
  275.1 3.1 %copy.13 = bf16[1,1024,1024]{2,1,0:T(8,128)(2,1)} copy(bf16[1,1024,1024]{2,1,0:T(8,128)(2,1)} %bitcast.7) | data formatting | bytes 4194304

commit v5 on v4

--- a/solution.py
+++ b/solution.py
@@ -115,8 +115,8 @@
             self.to_hub(n, N - 1).wait_send()
 
 
-def each(count, body):
-    lax.fori_loop(0, count, lambda i, _: (body(i), 0)[1], 0)
+def each(count, body, unroll=1):
+    lax.fori_loop(0, count, lambda i, _: (body(i), 0)[1], 0, unroll=unroll)
 
 
 def stage(c, body):
@@ -140,10 +140,10 @@
 
 def step_kernel(
     inv_ref, owner_ref, x_hbm, down_hbm, up_hbm, bias_ref, proj_hbm, cot_ref,
-    out_ref, inter_ref,
+    out_hbm, inter_ref,
     x_ref, map0, map1, map2, map3, proj_ref, ready, w_ref, pw_ref, bw_ref, cur, scales, grad,
     own, total_ref, mine, from_end, from_side, v_out, v_own, v_in, vg, ordered, got, back, ret,
-    bias_slots, picks, cots, tables,
+    bias_slots, picks, cots, tables, out_ref, out_sems,
     load_sems, sems, w_sems, v_sems, g_sems, t_sems,
 ):
     samples, width = x_ref.shape
@@ -340,7 +340,7 @@
                 device_id={"tower": other(d)},
             )
 
-        each(towers - 1, lambda d: copy(d).start())
+        each(towers - 1, lambda d: copy(d).start(), 9)
         dst[tower] = src[tower]
 
     def arrived(which, phase, ref):
@@ -419,6 +419,10 @@
             total = total + dot(dscale, ranks(w_ref, 1, lo, NB))
         line.put(3, c, total)
 
+    def out_copy(c):
+        rows = line.rows(c)
+        return pltpu.make_async_copy(out_ref.at[rows], out_hbm.at[rows], out_sems.at[c])
+
     def finish(c):
         rows = line.rows(c)
         line.get(3, c)
@@ -427,6 +431,7 @@
             cols = slice(lo, lo + NB)
             g0 = grad[rows, cols] + dot_t(dhidden, ranks(w_ref, 0, lo, NB))
             out_ref[rows, cols] = g0.astype(BF16)
+        out_copy(c).start()
 
     def both_sums(i):
         stage(i, last_layer)
@@ -437,6 +442,7 @@
 
     each(N + 6, both_sums)
 
+    each(N, lambda c: out_copy(c).wait())
     sent_w(3)
     for d in range(1, N):
         v_copy(me, (me + d) % N).wait_send()
@@ -453,7 +459,7 @@
 
 def params(collective_id):
     return pltpu.CompilerParams(
-        collective_id=collective_id, has_side_effects=True, vmem_limit_bytes=62 << 20
+        collective_id=collective_id, has_side_effects=True, vmem_limit_bytes=60 << 20
     )
 
 
@@ -477,7 +483,7 @@
             pl.BlockSpec(memory_space=pltpu.SMEM), vmem(), any_spec, any_spec, any_spec,
             vmem(), any_spec, vmem(),
         ],
-        out_specs=(vmem(),) * 2,
+        out_specs=(any_spec, vmem()),
         scratch_shapes=[
             pltpu.VMEM((samples, width), BF16),
             *[pltpu.VMEM((slots, E, E), BF16)] * 4,
@@ -499,6 +505,8 @@
             pltpu.VMEM((slots, 2, E), F32),
             pltpu.VMEM((2, 2 * block, block), BF16),
             *[pltpu.VMEM((2 * towers, inter_grad.shape[0], E), F32)] * 2,
+            pltpu.VMEM((samples, width), BF16),
+            dma((N,)),
             dma((6,)),
             dma((6, 4, N)),
             dma((2, 4, N)),

time: 278 us -> 279 us (level)
  no operation moved by 1% of the time
where the time goes in v5:
time: 279 us; the launch traced here: 278 us
  Pallas kernels  272 us (97%)
  local copies, waits for them, and re-layouts  4.75 us (2%)
    pallas_call x1, Pallas kernels, per_device(): pl.pallas_call(step_kernel, out_shape=(sds((samples, width), BF16), sds(i...  272 us

profile of v5, /device:TPU:2, one launch (start us, length us, event | category | flops | bytes accessed | tf_op | source)
XLA Modules:
  0.0 278.4 jit_solution(6067493480090327534)
XLA Ops:
  0.6 1.3 select_reduce_fusion.inv_ref
  1.9 271.7 %mega.1 = (bf16[1024,1024]{1,0:T(8,128)(2,1)}, f32[4,16384]{1,0:T(4,128)}) custom-call(s32[32]{0:T(128)} %select_reduce_fusion.inv_ref, s32[4,256]{1,0:T(4,128)} %owner_ref.1, bf16[1024,1024]{1,0:T(8,128)(2,1)} %bitcast.8, bf16[2,32,128,128]{3,2,1,0:T(8,128)(2,1)} %bitcast.9, bf16[2,32,128,128]{3,2,1,0:T(8,128)(2,1)} %bitcast.10, f32[2,4096]{1,0:T(2,128)} %bitcast.12, ...), custom_call_target="tpu_custom_call" | custom-call | tf_op jit(solution)/shard_map/mega/pallas_call | solution.py:479
  273.6 1.7 copy.12
  275.3 3.1 %copy.13 = bf16[1,1024,1024]{2,1,0:T(8,128)(2,1)} copy(bf16[1,1024,1024]{2,1,0:T(8,128)(2,1)} %bitcast.7) | data formatting | bytes 4194304

commit v6 on v5

--- a/solution.py
+++ b/solution.py
@@ -10,7 +10,7 @@
 E = 128
 N = 4
 PUMPS = ((1, 0), (2, 4), (3, 7))
-NB = 256
+NB = 512
 NT = (((1,), (1,)), ((), ()))
 TN = (((0,), (0,)), ((), ()))
 

time: 279 us -> 279 us (level)
  no operation moved by 1% of the time
where the time goes in v6:
time: 279 us; the launch traced here: 278 us
  Pallas kernels  272 us (97%)
  local copies, waits for them, and re-layouts  4.75 us (2%)
    pallas_call x1, Pallas kernels, per_device(): pl.pallas_call(step_kernel, out_shape=(sds((samples, width), BF16), sds(i...  272 us

profile of v6, /device:TPU:2, one launch (start us, length us, event | category | flops | bytes accessed | tf_op | source)
XLA Modules:
  0.0 278.4 jit_solution(16822629866011772284)
XLA Ops:
  0.6 1.3 select_reduce_fusion.inv_ref
  1.9 271.7 %mega.1 = (bf16[1024,1024]{1,0:T(8,128)(2,1)}, f32[4,16384]{1,0:T(4,128)}) custom-call(s32[32]{0:T(128)} %select_reduce_fusion.inv_ref, s32[4,256]{1,0:T(4,128)} %owner_ref.1, bf16[1024,1024]{1,0:T(8,128)(2,1)} %bitcast.8, bf16[2,32,128,128]{3,2,1,0:T(8,128)(2,1)} %bitcast.9, bf16[2,32,128,128]{3,2,1,0:T(8,128)(2,1)} %bitcast.10, f32[2,4096]{1,0:T(2,128)} %bitcast.12, ...), custom_call_target="tpu_custom_call" | custom-call | tf_op jit(solution)/shard_map/mega/pallas_call | solution.py:479
  273.6 1.7 copy.12
  275.3 3.1 %copy.13 = bf16[1,1024,1024]{2,1,0:T(8,128)(2,1)} copy(bf16[1,1024,1024]{2,1,0:T(8,128)(2,1)} %bitcast.7) | data formatting | bytes 4194304
